TPU v7x, 32 devices: a whole 2x2x4 slice. The times are simulated.
32 devices in a mesh: tm: 8 (over z, x), clip: 4 (over y, core).
Axes of the slice: x: 2, y: 2, z: 4, core: 2. Of those that a mesh axis runs over, the one named last changes fastest.
Arguments:
- video: float32 [4, 8, 16, 32, 320], P('clip', 'tm'), may hold values from -6 to 6
- spatial_w: bfloat16 [9, 320, 320], P(None, 'clip'), may hold values from -0.109375 to 0.109375
- spatial_b: float32 [320], replicated, may hold values from -3 to 3
- temporal_w: float32 [3, 320, 320], P(None, 'clip'), may hold values from -0.1875 to 0.1875
- cotangent: float32 [4, 8, 16, 32, 320], P('clip', 'tm'), may hold values from -6 to 6
Outputs:
- output: float32 [4, 8, 16, 32, 320], P('clip', 'tm')
- grad_video: float32 [4, 8, 16, 32, 320], P('clip', 'tm')
- grad_temporal: float32 [3, 320, 320], P(None, 'clip')
All inputs are finite; a program needn't handle non-finite values.
Results may differ from a plain program's by a relative error of at most 0.0049.
Values may be sent and summed in bfloat16 or wider, within the bound.
A program may use at most 64 MiB of HBM per device.

v0:
```python
import functools
import math

import jax
import jax.numpy as jnp
from jax import lax
from jax.experimental import pallas as pl
from jax.experimental.pallas import tpu as pltpu
from jax.sharding import PartitionSpec as P

F32 = jnp.float32
BF16 = jnp.bfloat16
MESH = pl.DeviceIdType.MESH


def nn_dot(left, right):
    return lax.dot_general(left, right, (((1,), (0,)), ((), ())), preferred_element_type=F32)


def outer_dot(left, right):
    return lax.dot_general(left, right, (((0,), (0,)), ((), ())), preferred_element_type=F32)


def transpose_dot(left, right):
    return lax.dot_general(left, right, (((1,), (1,)), ((), ())), preferred_element_type=F32)


def block_kernel(
    dims,
    video_h, sw_h, bias_ref, tw_h, cot_h,
    out_h, gv_h, gt_h,
    video, cot, sw, tw, wp, wg, xcat, cb, chalo, hb, hpack, hhalo, slope, gpad,
    out_v, gv_v, gt_v, gtl, rx, ysend, ry, psum, pb, rs, ag,
    load_sem, out_sem, w_send, w_recv, halo_send, halo_recv, g_send, g_recv, a_send, a_recv,
):
    n_tm, n_clip, height, width, chans, scale = dims
    rows = height * width
    depth = sw_h.shape[1]
    half = rows // 2
    quarter = rows // 4
    chunks = 4
    chunk = half // chunks
    tm = lax.axis_index("tm")
    c = lax.axis_index("clip")

    def flip(value, bit):
        return value + bit - 2 * bit * (lax.rem(value // bit, 2))

    core, ypart = flip(c, 1), flip(c, 2)
    xpart, zpart = flip(tm, 1), flip(tm, 2)
    parity = lax.rem(tm, 2)
    h = lax.rem(tm // 2, 2)

    barrier = pltpu.get_barrier_semaphore()
    for step in range(1, n_tm):
        pl.semaphore_signal(
            barrier, inc=1, device_id=(lax.rem(tm + step, n_tm), c), device_id_type=MESH
        )
    pl.semaphore_signal(barrier, inc=1, device_id=(tm, core), device_id_type=MESH)
    pl.semaphore_signal(barrier, inc=1, device_id=(tm, ypart), device_id_type=MESH)

    loads = [
        pltpu.make_async_copy(sw_h, sw, load_sem.at[0]),
        pltpu.make_async_copy(tw_h, tw, load_sem.at[1]),
        pltpu.make_async_copy(cot_h, cot, load_sem.at[2]),
        pltpu.make_async_copy(video_h, video, load_sem.at[3]),
    ]
    for load in loads:
        load.start()

    def pack(value):
        return jnp.concatenate([value[:quarter], value[quarter:]], axis=1)

    def unpack(ref, slot):
        parts = []
        for q in range(2):
            both = ref[slot, q * quarter : (q + 1) * quarter]
            parts += [both[:, :chans], both[:, chans:]]
        return jnp.concatenate(parts, axis=0)

    loads[0].wait()
    loads[1].wait()
    shard = [sw[tap] for tap in range(9)] + [tw[tap].astype(BF16) for tap in range(3)]
    for pair in range(6):
        wp[c, pair] = jnp.concatenate([shard[2 * pair], shard[2 * pair + 1]], axis=1)
    pl.semaphore_wait(barrier, n_tm + 1)

    def send(src, dst, ssem, rsem, device):
        copy = pltpu.make_async_remote_copy(
            src_ref=src, dst_ref=dst, send_sem=ssem, recv_sem=rsem,
            device_id=device, device_id_type=MESH,
        )
        copy.start()
        return copy

    def wsend(slot, owner, pair, device):
        part = wp.at[owner, pair]
        return send(part, part, w_send.at[slot], w_recv.at[slot], device)

    y_pairs = [parity, 2 + h, 4, 5]
    shared_pairs = [1 - parity, 3 - h]
    sharers = [(xpart, c), (zpart, c)]
    y_copies = [wsend(j, c, y_pairs[j], (tm, ypart)) for j in range(4)]
    own_copy = send(wp.at[c], wp.at[c], w_send.at[6], w_recv.at[6], (tm, core))

    loads[2].wait()
    own_cot = cot[...].astype(BF16)
    for q in range(2):
        cb[q * quarter : (q + 1) * quarter] = pack(own_cot[q * half : (q + 1) * half])

    def near_send(base, own, halo, q):
        part = pl.ds(q * chunk, chunk)
        return send(
            own.at[part, :], halo.at[parity, part, :],
            halo_send.at[base + q], halo_recv.at[base + q], (xpart, c),
        )

    def far_copy(base, halo, q):
        target = lax.rem(tm + n_tm + 2 - 4 * parity, n_tm)
        part = pl.ds(q * chunk, chunk)
        return pltpu.make_async_remote_copy(
            src_ref=halo.at[1 - parity, part, :],
            dst_ref=halo.at[parity, part, :],
            send_sem=halo_send.at[base + chunks + q],
            recv_sem=halo_recv.at[base + chunks + q],
            device_id=(target, c),
            device_id_type=MESH,
        )

    sends_far = jnp.logical_or(
        jnp.logical_and(parity == 0, tm + 2 < n_tm), jnp.logical_and(parity == 1, tm >= 2)
    )
    gets_far = jnp.logical_or(
        jnp.logical_and(parity == 0, tm >= 2), jnp.logical_and(parity == 1, tm + 2 < n_tm)
    )

    def far_start(base, halo, q):
        @pl.when(sends_far)
        def _():
            far_copy(base, halo, q).start()

    def far_recv(base, halo):
        @pl.when(gets_far)
        def _():
            for q in range(chunks):
                far_copy(base, halo, q).wait_recv()

    def far_done(base, halo):
        @pl.when(sends_far)
        def _():
            for q in range(chunks):
                far_copy(base, halo, q).wait_send()

    cot_near = [near_send(0, cb, chalo, q) for q in range(2)]

    for edge, slot in ((0, 0), (n_tm - 1, 1)):
        @pl.when(tm == edge)
        def _():
            chalo[slot] = jnp.zeros((half, 2 * chans), BF16)
            hhalo[slot] = jnp.zeros((half, 2 * chans), BF16)

    column = lax.rem(lax.broadcasted_iota(jnp.int32, (rows, chans), 0), width)

    def shifted(value, step):
        if step == 0:
            return value
        rolled = pltpu.roll(value, step % rows, 0)
        return jnp.where(column == (0 if step == 1 else width - 1), 0.0, rolled)

    xcat[0:width] = jnp.zeros((width, 3 * chans), BF16)
    xcat[width + rows :] = jnp.zeros((width, 3 * chans), BF16)
    for b in range(3):
        gpad[b, 0:width] = jnp.zeros((width, chans), BF16)
        gpad[b, width + rows :] = jnp.zeros((width, chans), BF16)
    loads[3].wait()
    frame = video[...]
    xcat[width : width + rows] = jnp.concatenate(
        [shifted(frame, 1).astype(BF16), frame.astype(BF16), shifted(frame, -1).astype(BF16)], axis=1
    )

    relays = []
    z_copies = []
    for j in range(2):
        y_copies[j].wait_recv()
        z_copies.append(wsend(4 + j, ypart, y_pairs[j], sharers[j]))
        if j == 0:
            cot_near += [near_send(0, cb, chalo, q) for q in range(2, chunks)]
        relays.append(wsend(7 + j, ypart, y_pairs[j], (tm, core)))
        cot_near[j].wait_recv()
        far_start(0, chalo, j)
    y_copies[2].wait_recv()
    relays.append(wsend(9, ypart, y_pairs[2], (tm, core)))
    for j in range(2):
        z_copies[j].wait_recv()
        relays.append(wsend(11 + j, ypart, shared_pairs[j], (tm, core)))
        cot_near[2 + j].wait_recv()
        far_start(0, chalo, 2 + j)
    own_copy.wait_recv()
    for copy in relays:
        copy.wait_recv()

    def unpack_weights(pair):
        for owner in range(n_clip):
            both = wp[owner, pair]
            band = slice(owner * depth, (owner + 1) * depth)
            wg[2 * pair, band] = both[:, :chans]
            wg[2 * pair + 1, band] = both[:, chans:]

    for pair in range(5):
        unpack_weights(pair)

    hid_near = []
    for q in range(2):
        acc = bias_ref[...].reshape(1, chans) + jnp.zeros((half, chans), F32)
        for a in range(3):
            acc = acc + nn_dot(
                xcat[a * width + q * half : a * width + (q + 1) * half],
                wg[3 * a : 3 * a + 3].reshape(3 * chans, chans),
            )
        sig = jax.nn.sigmoid(acc)
        hidden = (acc * sig).astype(BF16)
        hb[q * half : (q + 1) * half] = hidden
        hpack[q * quarter : (q + 1) * quarter] = pack(hidden)
        hid_near += [near_send(2 * chunks, hpack, hhalo, 2 * q + e) for e in range(2)]
        slope[q * half : (q + 1) * half] = sig * (1.0 + acc * (1.0 - sig))

    y_copies[3].wait_recv()
    relays.append(wsend(10, ypart, y_pairs[3], (tm, core)))

    lanes = psum.shape[2]
    wide = n_tm // 2 * lanes
    far_recv(0, chalo)
    hidden_all = hb[...]
    own_cot = cot[...].astype(BF16)
    before, after = unpack(chalo, 0), unpack(chalo, 1)
    products = jnp.concatenate(
        [outer_dot(hidden_all, right) for right in (after, own_cot, before)]
        + [jnp.zeros((chans, n_tm * lanes - 3 * chans), F32)],
        axis=1,
    )
    for owner in range(n_clip):
        gtl[owner % 2, owner // 2] = products[owner * depth : (owner + 1) * depth]
    yc = c // 2
    mine = lax.rem(c, 2)
    core_copies = [
        send(gtl.at[1 - mine, side], rx.at[side], g_send.at[e], g_recv.at[e], (tm, core))
        for e, side in enumerate((1 - yc, yc))
    ]

    def pass_hidden(q):
        hid_near[q].wait_recv()
        far_start(2 * chunks, hhalo, q)

    relays[-1].wait_recv()
    unpack_weights(5)
    grad_h = transpose_dot(after, wg[9]) + transpose_dot(own_cot, wg[10])
    grad_h = grad_h + transpose_dot(before, wg[11])
    pass_hidden(0)

    core_copies[0].wait_recv()
    y_sum = (gtl[mine, 1 - yc] + rx[1 - yc]).astype(BF16)
    grad_y = []
    for e in range(2):
        ysend[e] = y_sum[:, e * wide : (e + 1) * wide]
        grad_y.append(send(ysend.at[e], ry.at[e], g_send.at[2 + e], g_recv.at[2 + e], (tm, ypart)))

    grad_s = grad_h * slope[...]
    for b in range(3):
        gpad[b, width : width + rows] = shifted(grad_s, b - 1).astype(BF16)
    pass_hidden(1)
    pass_hidden(2)

    def grad_conv(q):
        acc = cot[q * half : (q + 1) * half]
        for a in range(3):
            start = (2 - a) * width + q * half
            for b in range(3):
                acc = acc + transpose_dot(gpad[b, start : start + half], wg[3 * a + b])
        gv_v[q * half : (q + 1) * half] = acc

    grad_conv(0)
    pass_hidden(3)

    core_copies[1].wait_recv()
    own_sum = gtl[mine, yc] + rx[yc]
    def scatter_copy(to):
        return pltpu.make_async_remote_copy(
            src_ref=pb.at[to], dst_ref=rs.at[tm], send_sem=a_send.at[to], recv_sem=a_recv.at[tm],
            device_id=(to, c), device_id_type=MESH,
        )

    def arrival(sender):
        return pltpu.make_async_remote_copy(
            src_ref=pb.at[sender], dst_ref=rs.at[sender], send_sem=a_send.at[sender],
            recv_sem=a_recv.at[sender], device_id=(sender, c), device_id_type=MESH,
        )

    for e in range(2):
        grad_y[e].wait_recv()
        both = own_sum[:, e * wide : (e + 1) * wide] + ry[e].astype(F32)
        for place in range(n_tm // 2):
            to = e * (n_tm // 2) + place
            part = both[:, place * lanes : (place + 1) * lanes]
            psum[to] = part
            pb[to] = part.astype(BF16)

            @pl.when(tm != to)
            def _():
                scatter_copy(to).start()

    grad_conv(1)
    gv_out = pltpu.make_async_copy(gv_v, gv_h, out_sem.at[0])
    gv_out.start()
    out_v[...] = video[...] + nn_dot(hb[...], wg[10])

    rs[tm] = jnp.zeros(rs.shape[1:], BF16)
    for sender in range(n_tm):
        @pl.when(tm != sender)
        def _():
            arrival(sender).wait_recv()
    total = psum[tm]
    for sender in range(n_tm):
        total = total + rs[sender].astype(F32)
    ag[tm] = total.astype(BF16)
    order = sorted(range(1, n_tm), key=lambda step: -min(step, n_tm - step))
    gathers = []
    for step in order:
        to = lax.rem(tm + step, n_tm)
        slot = n_tm - 1 + step
        gathers.append(send(ag.at[tm], ag.at[tm], a_send.at[slot], a_recv.at[slot], (to, c)))

    far_recv(2 * chunks, hhalo)
    out_v[...] = out_v[...] + nn_dot(unpack(hhalo, 0), wg[9]) + nn_dot(unpack(hhalo, 1), wg[11])
    out_out = pltpu.make_async_copy(out_v, out_h, out_sem.at[1])
    out_out.start()

    for copy in gathers:
        copy.wait_recv()
    whole = jnp.concatenate([ag[to] for to in range(n_tm)], axis=1).astype(F32) * scale
    for k in range(3):
        gt_v[k] = whole[:, k * chans : (k + 1) * chans]
    gt_out = pltpu.make_async_copy(gt_v, gt_h, out_sem.at[2])
    gt_out.start()

    for copy in (
        y_copies + z_copies + [own_copy] + relays + cot_near + hid_near
        + core_copies + grad_y + gathers
    ):
        copy.wait_send()
    far_done(0, chalo)
    far_done(2 * chunks, hhalo)
    for to in range(n_tm):
        @pl.when(tm != to)
        def _():
            arrival(to).wait_send()
    gv_out.wait()
    out_out.wait()
    gt_out.wait()


def hand_over(*refs):
    n = (len(refs) - 2) // 3
    ins, outs, held, (sem_in, sem_out) = refs[:n], refs[n : 2 * n], refs[2 * n : 3 * n], refs[3 * n :]
    reads, writes = [], []
    for e in range(n):
        extent = ins[e].shape[0]
        count = 4 if extent % 64 == 0 else 1
        for q in range(count):
            part = pl.ds(q * (extent // count), extent // count)
            slot = 4 * e + q
            reads.append(pltpu.make_async_copy(ins[e].at[part], held[e].at[part], sem_in.at[slot]))
            writes.append(pltpu.make_async_copy(held[e].at[part], outs[e].at[part], sem_out.at[slot]))
    for read in reads:
        read.start()
    for read, write in zip(reads, writes):
        read.wait()
        write.start()
    for write in writes:
        write.wait()


def fused(n_tm, n_clip, video, spatial_w, spatial_b, temporal_w, cotangent):
    clips, frames, height, width, chans = video.shape
    rows = height * width
    depth = spatial_w.shape[1]
    lanes = -(-3 * chans // (128 * n_tm)) * 128
    scale = 1.0 / math.sqrt(rows * n_tm * n_clip)
    any_spec = pl.BlockSpec(memory_space=pltpu.HBM)
    vm_spec = pl.BlockSpec(memory_space=pltpu.VMEM)
    vm = pltpu.VMEM
    dma = pltpu.SemaphoreType.DMA
    results = pl.pallas_call(
        functools.partial(block_kernel, (n_tm, n_clip, height, width, chans, scale)),
        out_shape=(
            jax.ShapeDtypeStruct((rows, chans), F32),
            jax.ShapeDtypeStruct((rows, chans), F32),
            jax.ShapeDtypeStruct((3, depth, chans), F32),
        ),
        in_specs=[any_spec, any_spec, vm_spec, any_spec, any_spec],
        out_specs=(any_spec, any_spec, any_spec),
        scratch_shapes=[
            vm((rows, chans), F32),
            vm((rows, chans), F32),
            vm((9, depth, chans), BF16),
            vm((3, depth, chans), F32),
            vm((n_clip, 6, depth, 2 * chans), BF16),
            vm((12, chans, chans), BF16),
            vm((rows + 2 * width, 3 * chans), BF16),
            vm((rows // 2, 2 * chans), BF16),
            vm((2, rows // 2, 2 * chans), BF16),
            vm((rows, chans), BF16),
            vm((rows // 2, 2 * chans), BF16),
            vm((2, rows // 2, 2 * chans), BF16),
            vm((rows, chans), F32),
            vm((3, rows + 2 * width, chans), BF16),
            vm((rows, chans), F32),
            vm((rows, chans), F32),
            vm((3, depth, chans), F32),
            vm((2, 2, depth, n_tm * lanes), F32),
            vm((2, depth, n_tm * lanes), F32),
            vm((2, depth, n_tm // 2 * lanes), BF16),
            vm((2, depth, n_tm // 2 * lanes), BF16),
            vm((n_tm, depth, lanes), F32),
            vm((n_tm, depth, lanes), BF16),
            vm((n_tm, depth, lanes), BF16),
            vm((n_tm, depth, lanes), BF16),
            dma((4,)),
            dma((3,)),
            dma((13,)),
            dma((13,)),
            dma((16,)),
            dma((16,)),
            dma((4,)),
            dma((4,)),
            dma((2 * n_tm,)),
            dma((2 * n_tm,)),
        ],
        compiler_params=pltpu.CompilerParams(
            collective_id=0, has_side_effects=True, vmem_limit_bytes=62 * 2**20
        ),
        name="block",
    )(
        video.reshape(rows, chans), spatial_w, spatial_b, temporal_w,
        cotangent.reshape(rows, chans),
    )
    shapes = tuple(jax.ShapeDtypeStruct(array.shape, F32) for array in results)
    out, gv, gt = pl.pallas_call(
        hand_over,
        out_shape=shapes,
        in_specs=[any_spec] * 3,
        out_specs=(any_spec,) * 3,
        scratch_shapes=[vm(shape.shape, F32) for shape in shapes] + [dma((12,)), dma((12,))],
        compiler_params=pltpu.CompilerParams(vmem_limit_bytes=62 * 2**20),
        name="hand_over",
    )(*results)
    return out.reshape(video.shape), gv.reshape(video.shape), gt


def padded_2(cells, sides, width):
    for axis, dim in sides:
        count = lax.axis_size(axis)
        ends = count - 1
        head = lax.slice_in_dim(cells, 0, width, axis=dim)
        tail = lax.slice_in_dim(cells, cells.shape[dim] - width, cells.shape[dim], axis=dim)
        cells = jnp.concatenate(
            [
                lax.ppermute(tail, axis, [(i, (i + 1) % count) for i in range(ends)]),
                cells,
                lax.ppermute(head, axis, [((i + 1) % count, i) for i in range(ends)]),
            ],
            axis=dim,
        )
    return cells


def native(video, spatial_w, spatial_b, temporal_w, cotangent):
    clips, frames, height, width, chans = video.shape
    row_count = clips * frames * height * width
    pads = ((0, 0), (0, 0), (1, 1), (1, 1), (0, 0))
    padded = jnp.pad(video.astype(BF16), pads)
    temporal_b = temporal_w.astype(BF16)
    spatial_all = lax.all_gather(spatial_w, "clip", axis=1, tiled=True)
    temporal_all = lax.all_gather(temporal_b, "clip", axis=1, tiled=True)
    spatial = jnp.zeros((row_count, chans), F32)
    for y in range(3):
        for x in range(3):
            window = padded[:, :, y : y + height, x : x + width, :].reshape(row_count, chans)
            spatial = spatial + nn_dot(window, spatial_all[3 * y + x])
    spatial = spatial + spatial_b
    sigmoid_s = jax.nn.sigmoid(spatial)
    hidden = (spatial * sigmoid_s).astype(BF16).reshape(video.shape)
    hidden_pad = padded_2(hidden, (("tm", 1),), 1)
    cot_b = cotangent.astype(BF16)
    cot_flat = cot_b.reshape(row_count, chans)
    cot_pad = padded_2(cot_b, (("tm", 1),), 1)
    temporal = jnp.zeros((row_count, chans), F32)
    grad_hidden = jnp.zeros((row_count, chans), F32)
    grads = []
    for k in range(3):
        shifted_hid = hidden_pad[:, k : k + frames].reshape(row_count, chans)
        temporal = temporal + nn_dot(shifted_hid, temporal_all[k])
        shifted_cot = cot_pad[:, 2 - k : 2 - k + frames].reshape(row_count, chans)
        grad_hidden = grad_hidden + transpose_dot(shifted_cot, temporal_all[k])
        grads.append(outer_dot(shifted_hid, cot_flat))
    total_rows = row_count * lax.axis_size("tm") * lax.axis_size("clip")
    summed = lax.psum(jnp.stack(grads), "tm")
    owned = lax.psum_scatter(summed, "clip", scatter_dimension=1, tiled=True)
    grad_spatial = (grad_hidden * sigmoid_s * (1.0 + spatial * (1.0 - sigmoid_s))).astype(BF16)
    grad_frames = jnp.pad(grad_spatial.reshape(video.shape), pads)
    grad_acc = cotangent.reshape(row_count, chans)
    for y in range(3):
        for x in range(3):
            window = grad_frames[:, :, 2 - y : 2 - y + height, 2 - x : 2 - x + width, :]
            window = window.reshape(row_count, chans)
            grad_acc = grad_acc + transpose_dot(window, spatial_all[3 * y + x])
    return (
        video + temporal.reshape(video.shape),
        grad_acc.reshape(video.shape),
        owned * (1.0 / math.sqrt(total_rows)),
    )


def solution(mesh):
    n_tm, n_clip = mesh.shape["tm"], mesh.shape["clip"]

    def on_device(video, spatial_w, spatial_b, temporal_w, cotangent):
        args = (video, spatial_w, spatial_b, temporal_w, cotangent)
        one_frame = video.shape[0] == 1 and video.shape[1] == 1
        if one_frame and spatial_w.shape[1] % 16 == 0 and n_clip == 4 and n_tm % 4 == 0:
            return fused(n_tm, n_clip, *args)
        return native(*args)

    return jax.shard_map(
        on_device,
        mesh=mesh,
        in_specs=(
            P("clip", "tm", None, None, None),
            P(None, "clip", None),
            P(),
            P(None, "clip", None),
            P("clip", "tm", None, None, None),
        ),
        out_specs=(
            P("clip", "tm", None, None, None),
            P("clip", "tm", None, None, None),
            P(None, "clip", None),
        ),
        check_vma=False,
    )
```

profile of v0, /device:TPU:0, one launch (start us, length us, event | category | flops | bytes accessed | tf_op | source)
XLA Modules:
  0.0 47.8 jit_solution(17540960912105228908)
XLA Ops:
  0.6 44.6 %block.1 = (f32[512,320]{1,0:T(8,128)}, f32[512,320]{1,0:T(8,128)}, f32[3,80,320]{2,1,0:T(8,128)}) custom-call(f32[512,320]{1,0:T(8,128)} %bitcast.4, bf16[9,80,320]{2,1,0:T(8,128)(2,1)} %sw_h.1, f32[320]{0:T(512)} %bias_ref.1, f32[3,80,320]{2,1,0:T(8,128)} %tw_h.1, f32[512,320]{1,0:T(8,128)} %bitcast.5), custom_call_target="tpu_custom_call" | custom-call | tf_op jit(solution)/shard_map/block/pallas_call | solution.py:392
  45.3 2.5 %hand_over.1 = (f32[512,320]{1,0:T(8,128)}, f32[512,320]{1,0:T(8,128)}, f32[3,80,320]{2,1,0:T(8,128)}) custom-call(f32[512,320]{1,0:T(8,128)} %get-tuple-element.9.refs_0_, f32[512,320]{1,0:T(8,128)} %get-tuple-element.10.refs_1_, f32[3,80,320]{2,1,0:T(8,128)} %get-tuple-element.11.refs_2_), custom_call_target="tpu_custom_call" | custom-call | tf_op jit(solution)/shard_map/hand_over/pallas_call | solution.py:447
where the time goes:
time: 48 us; the launch traced here: 47.8 us
  Pallas kernels  47.2 us (98%)
  between operations  0.64 us (1%)
    pallas_call x1, Pallas kernels, fused(): pl.pallas_call(functools.partial(block_kernel, (n_tm, n_clip, height, wid...  44.6 us
    pallas_call x1, Pallas kernels, fused(): pl.pallas_call(hand_over, out_shape=shapes, in_specs=[any_spec] * 3, out_...  2.53 us

commit v1 on v0

--- a/solution.py
+++ b/solution.py
@@ -27,11 +27,11 @@
 
 def block_kernel(
     dims,
-    video_h, sw_h, bias_ref, tw_h, cot_h,
-    out_h, gv_h, gt_h,
+    video_h, sw_h, bias_h, tw_h, cot_h,
+    out_v, gv_v, gt_v,
     video, cot, sw, tw, wp, wg, xcat, cb, chalo, hb, hpack, hhalo, slope, gpad,
-    out_v, gv_v, gt_v, gtl, rx, ysend, ry, psum, pb, rs, ag,
-    load_sem, out_sem, w_send, w_recv, halo_send, halo_recv, g_send, g_recv, a_send, a_recv,
+    bias_ref, gtl, rx, ysend, ry, psum, pb, rs, ag,
+    load_sem, w_send, w_recv, halo_send, halo_recv, g_send, g_recv, a_send, a_recv,
 ):
     n_tm, n_clip, height, width, chans, scale = dims
     rows = height * width
@@ -64,6 +64,7 @@
         pltpu.make_async_copy(tw_h, tw, load_sem.at[1]),
         pltpu.make_async_copy(cot_h, cot, load_sem.at[2]),
         pltpu.make_async_copy(video_h, video, load_sem.at[3]),
+        pltpu.make_async_copy(bias_h, bias_ref, load_sem.at[4]),
     ]
     for load in loads:
         load.start()
@@ -173,6 +174,7 @@
         gpad[b, 0:width] = jnp.zeros((width, chans), BF16)
         gpad[b, width + rows :] = jnp.zeros((width, chans), BF16)
     loads[3].wait()
+    loads[4].wait()
     frame = video[...]
     xcat[width : width + rows] = jnp.concatenate(
         [shifted(frame, 1).astype(BF16), frame.astype(BF16), shifted(frame, -1).astype(BF16)], axis=1
@@ -309,8 +311,6 @@
                 scatter_copy(to).start()
 
     grad_conv(1)
-    gv_out = pltpu.make_async_copy(gv_v, gv_h, out_sem.at[0])
-    gv_out.start()
     out_v[...] = video[...] + nn_dot(hb[...], wg[10])
 
     rs[tm] = jnp.zeros(rs.shape[1:], BF16)
@@ -331,16 +331,12 @@
 
     far_recv(2 * chunks, hhalo)
     out_v[...] = out_v[...] + nn_dot(unpack(hhalo, 0), wg[9]) + nn_dot(unpack(hhalo, 1), wg[11])
-    out_out = pltpu.make_async_copy(out_v, out_h, out_sem.at[1])
-    out_out.start()
 
     for copy in gathers:
         copy.wait_recv()
     whole = jnp.concatenate([ag[to] for to in range(n_tm)], axis=1).astype(F32) * scale
     for k in range(3):
         gt_v[k] = whole[:, k * chans : (k + 1) * chans]
-    gt_out = pltpu.make_async_copy(gt_v, gt_h, out_sem.at[2])
-    gt_out.start()
 
     for copy in (
         y_copies + z_copies + [own_copy] + relays + cot_near + hid_near
@@ -353,27 +349,19 @@
         @pl.when(tm != to)
         def _():
             arrival(to).wait_send()
-    gv_out.wait()
-    out_out.wait()
-    gt_out.wait()
 
 
 def hand_over(*refs):
-    n = (len(refs) - 2) // 3
-    ins, outs, held, (sem_in, sem_out) = refs[:n], refs[n : 2 * n], refs[2 * n : 3 * n], refs[3 * n :]
-    reads, writes = [], []
+    n = len(refs) // 2
+    ins, outs, sem = refs[:n], refs[n : 2 * n], refs[2 * n]
+    writes = []
     for e in range(n):
         extent = ins[e].shape[0]
         count = 4 if extent % 64 == 0 else 1
         for q in range(count):
             part = pl.ds(q * (extent // count), extent // count)
-            slot = 4 * e + q
-            reads.append(pltpu.make_async_copy(ins[e].at[part], held[e].at[part], sem_in.at[slot]))
-            writes.append(pltpu.make_async_copy(held[e].at[part], outs[e].at[part], sem_out.at[slot]))
-    for read in reads:
-        read.start()
-    for read, write in zip(reads, writes):
-        read.wait()
+            writes.append(pltpu.make_async_copy(ins[e].at[part], outs[e].at[part], sem.at[4 * e + q]))
+    for write in writes:
         write.start()
     for write in writes:
         write.wait()
@@ -392,12 +380,12 @@
     results = pl.pallas_call(
         functools.partial(block_kernel, (n_tm, n_clip, height, width, chans, scale)),
         out_shape=(
-            jax.ShapeDtypeStruct((rows, chans), F32),
-            jax.ShapeDtypeStruct((rows, chans), F32),
-            jax.ShapeDtypeStruct((3, depth, chans), F32),
+            vm((rows, chans), F32),
+            vm((rows, chans), F32),
+            vm((3, depth, chans), F32),
         ),
-        in_specs=[any_spec, any_spec, vm_spec, any_spec, any_spec],
-        out_specs=(any_spec, any_spec, any_spec),
+        in_specs=[any_spec, any_spec, any_spec, any_spec, any_spec],
+        out_specs=(vm_spec, vm_spec, vm_spec),
         scratch_shapes=[
             vm((rows, chans), F32),
             vm((rows, chans), F32),
@@ -413,9 +401,7 @@
             vm((2, rows // 2, 2 * chans), BF16),
             vm((rows, chans), F32),
             vm((3, rows + 2 * width, chans), BF16),
-            vm((rows, chans), F32),
-            vm((rows, chans), F32),
-            vm((3, depth, chans), F32),
+            vm((chans,), F32),
             vm((2, 2, depth, n_tm * lanes), F32),
             vm((2, depth, n_tm * lanes), F32),
             vm((2, depth, n_tm // 2 * lanes), BF16),
@@ -424,8 +410,7 @@
             vm((n_tm, depth, lanes), BF16),
             vm((n_tm, depth, lanes), BF16),
             vm((n_tm, depth, lanes), BF16),
-            dma((4,)),
-            dma((3,)),
+            dma((5,)),
             dma((13,)),
             dma((13,)),
             dma((16,)),
@@ -436,7 +421,7 @@
             dma((2 * n_tm,)),
         ],
         compiler_params=pltpu.CompilerParams(
-            collective_id=0, has_side_effects=True, vmem_limit_bytes=62 * 2**20
+            collective_id=0, has_side_effects=True, vmem_limit_bytes=65_000_000
         ),
         name="block",
     )(
@@ -444,13 +429,14 @@
         cotangent.reshape(rows, chans),
     )
     shapes = tuple(jax.ShapeDtypeStruct(array.shape, F32) for array in results)
+
     out, gv, gt = pl.pallas_call(
         hand_over,
         out_shape=shapes,
-        in_specs=[any_spec] * 3,
+        in_specs=[vm_spec] * 3,
         out_specs=(any_spec,) * 3,
-        scratch_shapes=[vm(shape.shape, F32) for shape in shapes] + [dma((12,)), dma((12,))],
-        compiler_params=pltpu.CompilerParams(vmem_limit_bytes=62 * 2**20),
+        scratch_shapes=[dma((12,))],
+        compiler_params=pltpu.CompilerParams(vmem_limit_bytes=2**20),
         name="hand_over",
     )(*results)
     return out.reshape(video.shape), gv.reshape(video.shape), gt

time: 48 us -> 45.5 us (0.948)
  Pallas kernels: 47.2 us -> 44.7 us
    pallas_call x1, Pallas kernels: 44.6 us -> 43.3 us  [fused(): pl.pallas_call(functools.partial(block_kernel, (n_tm, n_clip, height, wid...]
    pallas_call x1, Pallas kernels: 2.53 us -> 1.36 us  [fused(): pl.pallas_call(hand_over, out_shape=shapes, in_specs=[vm_spec] * 3, out_s...]
where the time goes in v1:
time: 45.5 us; the launch traced here: 45.3 us
  Pallas kernels  44.7 us (98%)
  between operations  0.64 us (1%)
    pallas_call x1, Pallas kernels, fused(): pl.pallas_call(functools.partial(block_kernel, (n_tm, n_clip, height, wid...  43.3 us
    pallas_call x1, Pallas kernels, fused(): pl.pallas_call(hand_over, out_shape=shapes, in_specs=[vm_spec] * 3, out_s...  1.36 us

profile of v1, /device:TPU:0, one launch (start us, length us, event | category | flops | bytes accessed | tf_op | source)
XLA Modules:
  0.0 45.3 jit_solution(7443309559745390694)
XLA Ops:
  0.6 43.3 %block.1 = (f32[512,320]{1,0:T(8,128)S(1)}, f32[512,320]{1,0:T(8,128)S(1)}, f32[3,80,320]{2,1,0:T(8,128)S(1)}) custom-call(f32[512,320]{1,0:T(8,128)} %bitcast.4, bf16[9,80,320]{2,1,0:T(8,128)(2,1)} %sw_h.1, f32[320]{0:T(512)} %bias_h.1, f32[3,80,320]{2,1,0:T(8,128)} %tw_h.1, f32[512,320]{1,0:T(8,128)} %bitcast.5), custom_call_target="tpu_custom_call" | custom-call | tf_op jit(solution)/shard_map/block/pallas_call | solution.py:380
  44.0 1.4 %hand_over.1 = (f32[512,320]{1,0:T(8,128)}, f32[512,320]{1,0:T(8,128)}, f32[3,80,320]{2,1,0:T(8,128)}) custom-call(f32[512,320]{1,0:T(8,128)S(1)} %get-tuple-element.9.refs_0_, f32[512,320]{1,0:T(8,128)S(1)} %get-tuple-element.10.refs_1_, f32[3,80,320]{2,1,0:T(8,128)S(1)} %get-tuple-element.11.refs_2_), custom_call_target="tpu_custom_call" | custom-call | tf_op jit(solution)/shard_map/hand_over/pallas_call | solution.py:433

commit v2 on v1

--- a/solution.py
+++ b/solution.py
@@ -25,21 +25,35 @@
     return lax.dot_general(left, right, (((1,), (1,)), ((), ())), preferred_element_type=F32)
 
 
+TAIL = 1
+
+
+def own_cot_of(ref):
+    return ref[...].astype(BF16)
+
+
 def block_kernel(
     dims,
     video_h, sw_h, bias_h, tw_h, cot_h,
     out_v, gv_v, gt_v,
-    video, cot, sw, tw, wp, wg, xcat, cb, chalo, hb, hpack, hhalo, slope, gpad,
-    bias_ref, gtl, rx, ysend, ry, psum, pb, rs, ag,
-    load_sem, w_send, w_recv, halo_send, halo_recv, g_send, g_recv, a_send, a_recv,
+    video, cot, sw, tw, bias_ref, wp, wg, xcat, cb, chalo, cote, cotl, hb, hpack, hhalo, stash, spat, gpad,
+    gtl, rx, ysend, ry, psum, pb, rs, ag,
+    load_sem, w_send, w_recv, halo_send, halo_recv, g_send, g_recv, a_send, a_recv, gate,
 ):
     n_tm, n_clip, height, width, chans, scale = dims
     rows = height * width
     depth = sw_h.shape[1]
     half = rows // 2
     quarter = rows // 4
+    side_chans = chans // 2
     chunks = 4
     chunk = half // chunks
+    low = depth - 16 * TAIL
+    head = -(-chans // 128) * 128
+    lanes = psum.shape[2]
+    n_early = 2 * chans // lanes
+    n_late = n_tm - n_early
+    skip = n_late * lanes - chans
     tm = lax.axis_index("tm")
     c = lax.axis_index("clip")
 
@@ -50,14 +64,41 @@
     xpart, zpart = flip(tm, 1), flip(tm, 2)
     parity = lax.rem(tm, 2)
     h = lax.rem(tm // 2, 2)
+    yc = c // 2
+    mine = lax.rem(c, 2)
+    has_up, has_down = tm + 2 < n_tm, tm >= 2
+
+    def signal(sem, device):
+        pl.semaphore_signal(sem, inc=1, device_id=device, device_id_type=MESH)
+
+    def tm_signals(sem):
+        signal(sem, (xpart, c))
+
+        @pl.when(has_up)
+        def _():
+            signal(sem, (tm + 2, c))
+
+        @pl.when(has_down)
+        def _():
+            signal(sem, (tm - 2, c))
+
+    def tm_waits(sem, extra):
+        n_z, z = n_tm // 2, tm // 2
+        ups, downs = (2 * n_z - 2 - z) // n_z, (z + n_z - 1) // n_z
+        pl.semaphore_wait(sem, 1 + extra + ups + downs)
+
+    rounds = n_tm // 2 - 1
+
+    def gate_step(r):
+        if r < rounds:
+            tm_waits(gate.at[r], 0)
+        if r + 1 < rounds:
+            tm_signals(gate.at[r + 1])
 
     barrier = pltpu.get_barrier_semaphore()
-    for step in range(1, n_tm):
-        pl.semaphore_signal(
-            barrier, inc=1, device_id=(lax.rem(tm + step, n_tm), c), device_id_type=MESH
-        )
-    pl.semaphore_signal(barrier, inc=1, device_id=(tm, core), device_id_type=MESH)
-    pl.semaphore_signal(barrier, inc=1, device_id=(tm, ypart), device_id_type=MESH)
+    signal(barrier, (tm, ypart))
+    signal(barrier, (tm, core))
+    tm_signals(barrier)
 
     loads = [
         pltpu.make_async_copy(sw_h, sw, load_sem.at[0]),
@@ -84,7 +125,7 @@
     shard = [sw[tap] for tap in range(9)] + [tw[tap].astype(BF16) for tap in range(3)]
     for pair in range(6):
         wp[c, pair] = jnp.concatenate([shard[2 * pair], shard[2 * pair + 1]], axis=1)
-    pl.semaphore_wait(barrier, n_tm + 1)
+    tm_waits(barrier, 2)
 
     def send(src, dst, ssem, rsem, device):
         copy = pltpu.make_async_remote_copy(
@@ -94,25 +135,42 @@
         copy.start()
         return copy
 
-    def wsend(slot, owner, pair, device):
-        part = wp.at[owner, pair]
-        return send(part, part, w_send.at[slot], w_recv.at[slot], device)
-
-    y_pairs = [parity, 2 + h, 4, 5]
-    shared_pairs = [1 - parity, 3 - h]
-    sharers = [(xpart, c), (zpart, c)]
-    y_copies = [wsend(j, c, y_pairs[j], (tm, ypart)) for j in range(4)]
-    own_copy = send(wp.at[c], wp.at[c], w_send.at[6], w_recv.at[6], (tm, core))
+    w_copies = []
+
+    def wsend(slot, part, device):
+        copy = send(part, part, w_send.at[slot], w_recv.at[slot], device)
+        w_copies.append(copy)
+        return copy
+
+    def low_part(owner, pair):
+        return wp.at[owner, pair, pl.ds(0, low)]
+
+    def rest_part(owner):
+        return wp.at[owner, pl.ds(0, 4), pl.ds(low, depth - low)]
+
+    def head_part(owner):
+        return wp.at[owner, 4, :, pl.ds(0, head)]
+
+    def tail_part(owner):
+        return wp.at[owner, 4, :, pl.ds(head, 2 * chans - head)]
+
+    at_y, at_core, at_x, at_z = (tm, ypart), (tm, core), (xpart, c), (zpart, c)
+    y_a = wsend(0, low_part(c, parity), at_y)
+    y_b = wsend(1, low_part(c, 2 + h), at_y)
+    y_rest = wsend(2, rest_part(c), at_y)
+    y_head = wsend(3, head_part(c), at_y)
+    own = wsend(8, wp.at[c, pl.ds(0, 5)], at_core)
+    tm_signals(gate.at[0])
 
     loads[2].wait()
     own_cot = cot[...].astype(BF16)
     for q in range(2):
         cb[q * quarter : (q + 1) * quarter] = pack(own_cot[q * half : (q + 1) * half])
 
-    def near_send(base, own, halo, q):
+    def near_send(base, own_ref, halo, q):
         part = pl.ds(q * chunk, chunk)
         return send(
-            own.at[part, :], halo.at[parity, part, :],
+            own_ref.at[part, :], halo.at[parity, part, :],
             halo_send.at[base + q], halo_recv.at[base + q], (xpart, c),
         )
 
@@ -129,10 +187,10 @@
         )
 
     sends_far = jnp.logical_or(
-        jnp.logical_and(parity == 0, tm + 2 < n_tm), jnp.logical_and(parity == 1, tm >= 2)
+        jnp.logical_and(parity == 0, has_up), jnp.logical_and(parity == 1, has_down)
     )
     gets_far = jnp.logical_or(
-        jnp.logical_and(parity == 0, tm >= 2), jnp.logical_and(parity == 1, tm + 2 < n_tm)
+        jnp.logical_and(parity == 0, has_down), jnp.logical_and(parity == 1, has_up)
     )
 
     def far_start(base, halo, q):
@@ -168,109 +226,246 @@
         rolled = pltpu.roll(value, step % rows, 0)
         return jnp.where(column == (0 if step == 1 else width - 1), 0.0, rolled)
 
-    xcat[0:width] = jnp.zeros((width, 3 * chans), BF16)
-    xcat[width + rows :] = jnp.zeros((width, 3 * chans), BF16)
+    for s in range(2):
+        xcat[s, 0:width] = jnp.zeros((width, 3 * side_chans), BF16)
+        xcat[s, width + rows :] = jnp.zeros((width, 3 * side_chans), BF16)
     for b in range(3):
         gpad[b, 0:width] = jnp.zeros((width, chans), BF16)
         gpad[b, width + rows :] = jnp.zeros((width, chans), BF16)
     loads[3].wait()
     loads[4].wait()
     frame = video[...]
-    xcat[width : width + rows] = jnp.concatenate(
-        [shifted(frame, 1).astype(BF16), frame.astype(BF16), shifted(frame, -1).astype(BF16)], axis=1
-    )
-
-    relays = []
-    z_copies = []
-    for j in range(2):
-        y_copies[j].wait_recv()
-        z_copies.append(wsend(4 + j, ypart, y_pairs[j], sharers[j]))
-        if j == 0:
-            cot_near += [near_send(0, cb, chalo, q) for q in range(2, chunks)]
-        relays.append(wsend(7 + j, ypart, y_pairs[j], (tm, core)))
-        cot_near[j].wait_recv()
-        far_start(0, chalo, j)
-    y_copies[2].wait_recv()
-    relays.append(wsend(9, ypart, y_pairs[2], (tm, core)))
-    for j in range(2):
-        z_copies[j].wait_recv()
-        relays.append(wsend(11 + j, ypart, shared_pairs[j], (tm, core)))
-        cot_near[2 + j].wait_recv()
-        far_start(0, chalo, 2 + j)
-    own_copy.wait_recv()
-    for copy in relays:
+    views = [shifted(frame, 1 - b).astype(BF16) for b in range(3)]
+    for s in range(2):
+        xcat[s, width : width + rows] = jnp.concatenate(
+            [view[:, s * side_chans : (s + 1) * side_chans] for view in views], axis=1
+        )
+
+    def unpack_pair(owner, pair, taps=(0, 1)):
+        both = wp[owner, pair] if 1 in taps else wp[owner, pair, :, 0:head]
+        band = pl.ds(pl.multiple_of(owner * depth, 16), depth)
+        for e in taps:
+            wg[2 * pair + e, band] = both[:, e * chans : (e + 1) * chans]
+
+    def unpack_spatial(owner):
+        for pair in range(4):
+            unpack_pair(owner, pair)
+        unpack_pair(owner, 4, (0,))
+
+    def conv_part(s, q):
+        total = None
+        for a in range(3):
+            band = pl.ds(pl.multiple_of(s * side_chans, 16), side_chans)
+            weights = jnp.concatenate([wg[3 * a + b, band] for b in range(3)], axis=0)
+            term = nn_dot(
+                xcat[s, a * width + q * half : a * width + (q + 1) * half], weights
+            )
+            total = term if total is None else total + term
+        return total
+
+    unpack_spatial(c)
+
+    @pl.when(parity == 0)
+    def _():
+        cote[:, chans : 2 * chans] = own_cot_of(cot)
+        cotl[:, chans:] = jnp.zeros((rows, skip), BF16)
+
+    @pl.when(parity == 1)
+    def _():
+        middle = own_cot_of(cot)
+        cote[:, 0 : chans - skip] = middle[:, skip:]
+        cote[:, 2 * chans - skip :] = jnp.zeros((rows, skip), BF16)
+        cotl[:, chans:] = middle[:, :skip]
+
+    own.wait_recv()
+    unpack_spatial(core)
+    for q in range(2):
+        spat[q * half : (q + 1) * half] = bias_ref[...].reshape(1, chans) + conv_part(yc, q)
+
+    y_a.wait_recv()
+    x_a = wsend(6, low_part(ypart, parity), at_x)
+    r_a = wsend(10, low_part(ypart, parity), at_core)
+    cot_near += [near_send(0, cb, chalo, q) for q in range(2, chunks)]
+    cot_near[0].wait_recv()
+    far_start(0, chalo, 0)
+    y_b.wait_recv()
+    z_b = wsend(7, low_part(ypart, 2 + h), at_z)
+    r_b = wsend(11, low_part(ypart, 2 + h), at_core)
+    cot_near[1].wait_recv()
+    far_start(0, chalo, 1)
+    gate_step(0)
+    y_rest.wait_recv()
+    r_rest = wsend(12, rest_part(ypart), at_core)
+    y_tail = wsend(4, tail_part(c), at_y)
+    y_last = wsend(5, wp.at[c, 5], at_y)
+    own_last = wsend(9, wp.at[c, 5], at_core)
+    x_a.wait_recv()
+    r_x = wsend(14, low_part(ypart, 1 - parity), at_core)
+    gate_step(1)
+    y_head.wait_recv()
+    r_head = wsend(13, head_part(ypart), at_core)
+    z_b.wait_recv()
+    r_z = wsend(15, low_part(ypart, 3 - h), at_core)
+    unpack_spatial(ypart)
+    cot_near[2].wait_recv()
+    far_start(0, chalo, 2)
+    for copy in (r_a, r_b, r_rest, r_x, r_head, r_z):
         copy.wait_recv()
-
-    def unpack_weights(pair):
-        for owner in range(n_clip):
-            both = wp[owner, pair]
-            band = slice(owner * depth, (owner + 1) * depth)
-            wg[2 * pair, band] = both[:, :chans]
-            wg[2 * pair + 1, band] = both[:, chans:]
-
-    for pair in range(5):
-        unpack_weights(pair)
+    unpack_spatial(flip(core, 2))
+
+    def stash_copy(q):
+        part = pl.ds(q * chunk, chunk)
+        return pltpu.make_async_remote_copy(
+            src_ref=hpack.at[part, :], dst_ref=stash.at[part, :],
+            send_sem=halo_send.at[4 * chunks + q], recv_sem=halo_recv.at[4 * chunks + q],
+            device_id=(lax.rem(tm + n_tm + 4 * parity - 2, n_tm), c), device_id_type=MESH,
+        )
+
+    def forward_copy(q):
+        part = pl.ds(q * chunk, chunk)
+        return pltpu.make_async_remote_copy(
+            src_ref=stash.at[part, :], dst_ref=hhalo.at[1 - parity, part, :],
+            send_sem=halo_send.at[3 * chunks + q], recv_sem=halo_recv.at[3 * chunks + q],
+            device_id=at_x, device_id_type=MESH,
+        )
+
+    def stash_hidden(q):
+        @pl.when(gets_far)
+        def _():
+            stash_copy(q).start()
+
+    def forward_hidden(q):
+        @pl.when(sends_far)
+        def _():
+            stash_copy(q).wait_recv()
+            forward_copy(q).start()
 
     hid_near = []
     for q in range(2):
-        acc = bias_ref[...].reshape(1, chans) + jnp.zeros((half, chans), F32)
-        for a in range(3):
-            acc = acc + nn_dot(
-                xcat[a * width + q * half : a * width + (q + 1) * half],
-                wg[3 * a : 3 * a + 3].reshape(3 * chans, chans),
-            )
-        sig = jax.nn.sigmoid(acc)
-        hidden = (acc * sig).astype(BF16)
+        acc = spat[q * half : (q + 1) * half] + conv_part(1 - yc, q)
+        hidden = (acc * jax.nn.sigmoid(acc)).astype(BF16)
         hb[q * half : (q + 1) * half] = hidden
         hpack[q * quarter : (q + 1) * quarter] = pack(hidden)
         hid_near += [near_send(2 * chunks, hpack, hhalo, 2 * q + e) for e in range(2)]
-        slope[q * half : (q + 1) * half] = sig * (1.0 + acc * (1.0 - sig))
-
-    y_copies[3].wait_recv()
-    relays.append(wsend(10, ypart, y_pairs[3], (tm, core)))
-
-    lanes = psum.shape[2]
-    wide = n_tm // 2 * lanes
-    far_recv(0, chalo)
-    hidden_all = hb[...]
-    own_cot = cot[...].astype(BF16)
-    before, after = unpack(chalo, 0), unpack(chalo, 1)
-    products = jnp.concatenate(
-        [outer_dot(hidden_all, right) for right in (after, own_cot, before)]
-        + [jnp.zeros((chans, n_tm * lanes - 3 * chans), F32)],
-        axis=1,
-    )
-    for owner in range(n_clip):
-        gtl[owner % 2, owner // 2] = products[owner * depth : (owner + 1) * depth]
-    yc = c // 2
-    mine = lax.rem(c, 2)
-    core_copies = [
-        send(gtl.at[1 - mine, side], rx.at[side], g_send.at[e], g_recv.at[e], (tm, core))
-        for e, side in enumerate((1 - yc, yc))
-    ]
+        if q == 1:
+            stash_hidden(2)
+            stash_hidden(3)
+        spat[q * half : (q + 1) * half] = acc
+        if q == 0:
+            cot_near[3].wait_recv()
+            far_start(0, chalo, 3)
+
+    early = (n_tm - n_early) * parity
+    late = n_early * (1 - parity)
+
+    def place(products, first, count):
+        for i in range(count):
+            for owner in range(n_clip):
+                gtl[owner % 2, owner // 2, first + i] = products[
+                    owner * depth : (owner + 1) * depth, i * lanes : (i + 1) * lanes
+                ]
+
+    def core_send(slot, side, first, count):
+        part = pl.ds(first, count)
+        return send(
+            gtl.at[1 - mine, side, part], rx.at[side, part],
+            g_send.at[slot], g_recv.at[slot], at_core,
+        )
+
+    def y_send(slot, first, count):
+        for i in range(count):
+            ysend[first + i] = (gtl[mine, 1 - yc, first + i] + rx[1 - yc, first + i]).astype(BF16)
+        part = pl.ds(first, count)
+        return send(ysend.at[part], ry.at[part], g_send.at[slot], g_recv.at[slot], at_y)
+
+    share = n_tm // 4
+    first_owner = n_tm // 2 - 2
+    owns = jnp.logical_and(tm >= first_owner, tm < first_owner + 4)
+
+    def scatter_copy(unit):
+        place_in = lax.rem(unit, share)
+        return pltpu.make_async_remote_copy(
+            src_ref=pb.at[unit], dst_ref=rs.at[tm, place_in],
+            send_sem=a_send.at[unit], recv_sem=a_recv.at[tm * share + place_in],
+            device_id=(first_owner + unit // share, c), device_id_type=MESH,
+        )
+
+    def arrival(sender, place_in):
+        return pltpu.make_async_remote_copy(
+            src_ref=pb.at[place_in], dst_ref=rs.at[sender, place_in], send_sem=a_send.at[place_in],
+            recv_sem=a_recv.at[sender * share + place_in],
+            device_id=(sender, c), device_id_type=MESH,
+        )
+
+    def gather_copy(owner, to):
+        part = ag.at[pl.ds(owner * share, share)]
+        return pltpu.make_async_remote_copy(
+            src_ref=part, dst_ref=part,
+            send_sem=a_send.at[n_tm + to], recv_sem=a_recv.at[n_tm * share + owner],
+            device_id=(to, c), device_id_type=MESH,
+        )
+
+    def scatter(first, count):
+        for i in range(count):
+            to = first + i
+            part = gtl[mine, yc, to] + rx[yc, to] + ry[to].astype(F32)
+            psum[to] = part
+            pb[to] = part.astype(BF16)
+
+            @pl.when(tm != first_owner + to // share)
+            def _():
+                scatter_copy(to).start()
 
     def pass_hidden(q):
         hid_near[q].wait_recv()
         far_start(2 * chunks, hhalo, q)
 
-    relays[-1].wait_recv()
-    unpack_weights(5)
-    grad_h = transpose_dot(after, wg[9]) + transpose_dot(own_cot, wg[10])
-    grad_h = grad_h + transpose_dot(before, wg[11])
+    @pl.when(parity == 0)
+    def _():
+        cote[:, 0:chans] = unpack(chalo, 1)
+
+    @pl.when(parity == 1)
+    def _():
+        cote[:, chans - skip : 2 * chans - skip] = unpack(chalo, 0)
+
+    place(outer_dot(hb[...], cote[...]), early, n_early)
+    core_e = [core_send(e, side, early, n_early) for e, side in enumerate((1 - yc, yc))]
+    core_e[0].wait_recv()
+    y_e = y_send(4, early, n_early)
+
+    far_recv(0, chalo)
+    cotl[:, 0:chans] = unpack(chalo, parity)
+    place(outer_dot(hb[...], cotl[...]), late, n_late)
+    core_l = [core_send(2 + e, side, late, n_late) for e, side in enumerate((1 - yc, yc))]
+
+    y_tail.wait_recv()
+    r_tail = wsend(16, tail_part(ypart), at_core)
+    y_last.wait_recv()
+    r_last = wsend(17, wp.at[ypart, 5], at_core)
     pass_hidden(0)
-
-    core_copies[0].wait_recv()
-    y_sum = (gtl[mine, 1 - yc] + rx[1 - yc]).astype(BF16)
-    grad_y = []
-    for e in range(2):
-        ysend[e] = y_sum[:, e * wide : (e + 1) * wide]
-        grad_y.append(send(ysend.at[e], ry.at[e], g_send.at[2 + e], g_recv.at[2 + e], (tm, ypart)))
-
-    grad_s = grad_h * slope[...]
+    core_l[0].wait_recv()
+    y_l = y_send(5, late, n_late)
+
+    for copy in (own_last, r_tail, r_last):
+        copy.wait_recv()
+    for owner in range(n_clip):
+        unpack_pair(owner, 4, (1,))
+        unpack_pair(owner, 5)
+    grad_h = transpose_dot(unpack(chalo, 1), wg[9])
+    grad_h = grad_h + transpose_dot(cot[...].astype(BF16), wg[10])
+    grad_h = grad_h + transpose_dot(unpack(chalo, 0), wg[11])
+    acc = spat[...]
+    sig = jax.nn.sigmoid(acc)
+    grad_s = grad_h * (sig * (1.0 + acc * (1.0 - sig)))
     for b in range(3):
         gpad[b, width : width + rows] = shifted(grad_s, b - 1).astype(BF16)
+
+    for r in range(2, rounds):
+        gate_step(r)
+    core_e[1].wait_recv()
+    y_e.wait_recv()
+    scatter(early, n_early)
     pass_hidden(1)
-    pass_hidden(2)
 
     def grad_conv(q):
         acc = cot[q * half : (q + 1) * half]
@@ -280,75 +475,74 @@
                 acc = acc + transpose_dot(gpad[b, start : start + half], wg[3 * a + b])
         gv_v[q * half : (q + 1) * half] = acc
 
+    core_l[1].wait_recv()
+    y_l.wait_recv()
+    scatter(late, n_late)
+    forward_hidden(2)
+    forward_hidden(3)
     grad_conv(0)
-    pass_hidden(3)
-
-    core_copies[1].wait_recv()
-    own_sum = gtl[mine, yc] + rx[yc]
-    def scatter_copy(to):
-        return pltpu.make_async_remote_copy(
-            src_ref=pb.at[to], dst_ref=rs.at[tm], send_sem=a_send.at[to], recv_sem=a_recv.at[tm],
-            device_id=(to, c), device_id_type=MESH,
-        )
-
-    def arrival(sender):
-        return pltpu.make_async_remote_copy(
-            src_ref=pb.at[sender], dst_ref=rs.at[sender], send_sem=a_send.at[sender],
-            recv_sem=a_recv.at[sender], device_id=(sender, c), device_id_type=MESH,
-        )
-
-    for e in range(2):
-        grad_y[e].wait_recv()
-        both = own_sum[:, e * wide : (e + 1) * wide] + ry[e].astype(F32)
-        for place in range(n_tm // 2):
-            to = e * (n_tm // 2) + place
-            part = both[:, place * lanes : (place + 1) * lanes]
-            psum[to] = part
-            pb[to] = part.astype(BF16)
-
+    grad_conv(1)
+    out_v[...] = video[...] + nn_dot(hb[...], wg[10])
+
+    @pl.when(owns)
+    def _():
+        mine_at = tm - first_owner
+        rs[tm] = jnp.zeros(rs.shape[1:], BF16)
+        for sender in range(n_tm):
+            @pl.when(tm != sender)
+            def _():
+                for e in range(share):
+                    arrival(sender, e).wait_recv()
+        for e in range(share):
+            total = psum[mine_at * share + e]
+            for sender in range(n_tm):
+                total = total + rs[sender, e].astype(F32)
+            ag[mine_at * share + e] = total.astype(BF16)
+        for to in (0, 1, n_tm - 2, n_tm - 1, *range(2, n_tm - 2)):
             @pl.when(tm != to)
             def _():
-                scatter_copy(to).start()
-
-    grad_conv(1)
-    out_v[...] = video[...] + nn_dot(hb[...], wg[10])
-
-    rs[tm] = jnp.zeros(rs.shape[1:], BF16)
-    for sender in range(n_tm):
-        @pl.when(tm != sender)
-        def _():
-            arrival(sender).wait_recv()
-    total = psum[tm]
-    for sender in range(n_tm):
-        total = total + rs[sender].astype(F32)
-    ag[tm] = total.astype(BF16)
-    order = sorted(range(1, n_tm), key=lambda step: -min(step, n_tm - step))
-    gathers = []
-    for step in order:
-        to = lax.rem(tm + step, n_tm)
-        slot = n_tm - 1 + step
-        gathers.append(send(ag.at[tm], ag.at[tm], a_send.at[slot], a_recv.at[slot], (to, c)))
+                gather_copy(mine_at, to).start()
 
     far_recv(2 * chunks, hhalo)
+    hid_near[2].wait_recv()
+    hid_near[3].wait_recv()
     out_v[...] = out_v[...] + nn_dot(unpack(hhalo, 0), wg[9]) + nn_dot(unpack(hhalo, 1), wg[11])
 
-    for copy in gathers:
-        copy.wait_recv()
+    for owner in range(4):
+        @pl.when(tm != first_owner + owner)
+        def _():
+            gather_copy(owner, tm).wait_recv()
     whole = jnp.concatenate([ag[to] for to in range(n_tm)], axis=1).astype(F32) * scale
     for k in range(3):
         gt_v[k] = whole[:, k * chans : (k + 1) * chans]
 
-    for copy in (
-        y_copies + z_copies + [own_copy] + relays + cot_near + hid_near
-        + core_copies + grad_y + gathers
-    ):
+    for copy in w_copies + cot_near + hid_near + core_e + core_l + [y_e, y_l]:
         copy.wait_send()
     far_done(0, chalo)
-    far_done(2 * chunks, hhalo)
-    for to in range(n_tm):
-        @pl.when(tm != to)
-        def _():
-            arrival(to).wait_send()
+
+    @pl.when(sends_far)
+    def _():
+        for q in range(2):
+            far_copy(2 * chunks, hhalo, q).wait_send()
+        for q in range(2, chunks):
+            forward_copy(q).wait_send()
+
+    @pl.when(gets_far)
+    def _():
+        for q in range(2, chunks):
+            stash_copy(q).wait_send()
+
+    for unit in range(n_tm):
+        @pl.when(tm != first_owner + unit // share)
+        def _():
+            scatter_copy(unit).wait_send()
+
+    @pl.when(owns)
+    def _():
+        for to in range(n_tm):
+            @pl.when(tm != to)
+            def _():
+                gather_copy(tm - first_owner, to).wait_send()
 
 
 def hand_over(*refs):
@@ -391,34 +585,38 @@
             vm((rows, chans), F32),
             vm((9, depth, chans), BF16),
             vm((3, depth, chans), F32),
+            vm((chans,), F32),
             vm((n_clip, 6, depth, 2 * chans), BF16),
             vm((12, chans, chans), BF16),
-            vm((rows + 2 * width, 3 * chans), BF16),
+            vm((2, rows + 2 * width, 3 * chans // 2), BF16),
             vm((rows // 2, 2 * chans), BF16),
             vm((2, rows // 2, 2 * chans), BF16),
+            vm((rows, 2 * chans), BF16),
+            vm((rows, n_tm * lanes - 2 * chans), BF16),
             vm((rows, chans), BF16),
             vm((rows // 2, 2 * chans), BF16),
             vm((2, rows // 2, 2 * chans), BF16),
+            vm((rows // 2, 2 * chans), BF16),
             vm((rows, chans), F32),
             vm((3, rows + 2 * width, chans), BF16),
-            vm((chans,), F32),
-            vm((2, 2, depth, n_tm * lanes), F32),
-            vm((2, depth, n_tm * lanes), F32),
-            vm((2, depth, n_tm // 2 * lanes), BF16),
-            vm((2, depth, n_tm // 2 * lanes), BF16),
+            vm((2, 2, n_tm, depth, lanes), F32),
+            vm((2, n_tm, depth, lanes), F32),
+            vm((n_tm, depth, lanes), BF16),
+            vm((n_tm, depth, lanes), BF16),
             vm((n_tm, depth, lanes), F32),
             vm((n_tm, depth, lanes), BF16),
-            vm((n_tm, depth, lanes), BF16),
+            vm((n_tm, n_tm // 4, depth, lanes), BF16),
             vm((n_tm, depth, lanes), BF16),
             dma((5,)),
-            dma((13,)),
-            dma((13,)),
-            dma((16,)),
-            dma((16,)),
-            dma((4,)),
-            dma((4,)),
+            dma((18,)),
+            dma((18,)),
+            dma((20,)),
+            dma((20,)),
+            dma((6,)),
+            dma((6,)),
             dma((2 * n_tm,)),
-            dma((2 * n_tm,)),
+            dma((n_tm * (n_tm // 4) + 4,)),
+            pltpu.SemaphoreType.REGULAR((n_tm // 2 - 1,)),
         ],
         compiler_params=pltpu.CompilerParams(
             collective_id=0, has_side_effects=True, vmem_limit_bytes=65_000_000
@@ -512,7 +710,10 @@
     def on_device(video, spatial_w, spatial_b, temporal_w, cotangent):
         args = (video, spatial_w, spatial_b, temporal_w, cotangent)
         one_frame = video.shape[0] == 1 and video.shape[1] == 1
-        if one_frame and spatial_w.shape[1] % 16 == 0 and n_clip == 4 and n_tm % 4 == 0:
+        depth, chans = spatial_w.shape[1:]
+        lanes = -(-3 * chans // (128 * n_tm)) * 128
+        fits = depth % 16 == 0 and depth > 16 * TAIL and 2 * chans % lanes == 0
+        if one_frame and fits and n_clip == 4 and n_tm % 4 == 0 and n_tm * lanes <= 4 * chans:
             return fused(n_tm, n_clip, *args)
         return native(*args)
 

time: 45.5 us -> 38.2 us (0.84)
  Pallas kernels: 44.7 us -> 37.4 us
    pallas_call x1, Pallas kernels: 43.3 us -> 36 us  [fused(): pl.pallas_call(functools.partial(block_kernel, (n_tm, n_clip, height, wid...]
where the time goes in v2:
time: 38.2 us; the launch traced here: 38 us
  Pallas kernels  37.4 us (98%)
  between operations  0.64 us (2%)
    pallas_call x1, Pallas kernels, fused(): pl.pallas_call(functools.partial(block_kernel, (n_tm, n_clip, height, wid...  36 us
    pallas_call x1, Pallas kernels, fused(): pl.pallas_call(hand_over, out_shape=shapes, in_specs=[vm_spec] * 3, out_s...  1.36 us

profile of v2, /device:TPU:0, one launch (start us, length us, event | category | flops | bytes accessed | tf_op | source)
XLA Modules:
  0.0 38.0 jit_solution(15829488193348206484)
XLA Ops:
  0.6 36.0 %block.1 = (f32[512,320]{1,0:T(8,128)S(1)}, f32[512,320]{1,0:T(8,128)S(1)}, f32[3,80,320]{2,1,0:T(8,128)S(1)}) custom-call(f32[512,320]{1,0:T(8,128)} %bitcast.4, bf16[9,80,320]{2,1,0:T(8,128)(2,1)} %sw_h.1, f32[320]{0:T(512)} %bias_h.1, f32[3,80,320]{2,1,0:T(8,128)} %tw_h.1, f32[512,320]{1,0:T(8,128)} %bitcast.5), custom_call_target="tpu_custom_call" | custom-call | tf_op jit(solution)/shard_map/block/pallas_call | solution.py:574
  36.7 1.4 %hand_over.1 = (f32[512,320]{1,0:T(8,128)}, f32[512,320]{1,0:T(8,128)}, f32[3,80,320]{2,1,0:T(8,128)}) custom-call(f32[512,320]{1,0:T(8,128)S(1)} %get-tuple-element.9.refs_0_, f32[512,320]{1,0:T(8,128)S(1)} %get-tuple-element.10.refs_1_, f32[3,80,320]{2,1,0:T(8,128)S(1)} %get-tuple-element.11.refs_2_), custom_call_target="tpu_custom_call" | custom-call | tf_op jit(solution)/shard_map/hand_over/pallas_call | solution.py:631

commit v3 on v2

--- a/solution.py
+++ b/solution.py
@@ -25,7 +25,7 @@
     return lax.dot_general(left, right, (((1,), (1,)), ((), ())), preferred_element_type=F32)
 
 
-TAIL = 1
+TAIL = 2
 
 
 def own_cot_of(ref):
@@ -36,7 +36,7 @@
     dims,
     video_h, sw_h, bias_h, tw_h, cot_h,
     out_v, gv_v, gt_v,
-    video, cot, sw, tw, bias_ref, wp, wg, xcat, cb, chalo, cote, cotl, hb, hpack, hhalo, stash, spat, gpad,
+    video, cot, sw, tw, bias_ref, wp, wg, xcat, cb, chalo, cote, cotl, hb, cstash, hpack, hhalo, hstash, spat, gpad,
     gtl, rx, ysend, ry, psum, pb, rs, ag,
     load_sem, w_send, w_recv, halo_send, halo_recv, g_send, g_recv, a_send, a_recv, gate,
 ):
@@ -101,7 +101,9 @@
     tm_signals(barrier)
 
     loads = [
-        pltpu.make_async_copy(sw_h, sw, load_sem.at[0]),
+        pltpu.make_async_copy(sw_h.at[pl.ds(0, 4)], sw.at[pl.ds(0, 4)], load_sem.at[0]),
+        pltpu.make_async_copy(sw_h.at[pl.ds(4, 4)], sw.at[pl.ds(4, 4)], load_sem.at[5]),
+        pltpu.make_async_copy(sw_h.at[pl.ds(8, 1)], sw.at[pl.ds(8, 1)], load_sem.at[6]),
         pltpu.make_async_copy(tw_h, tw, load_sem.at[1]),
         pltpu.make_async_copy(cot_h, cot, load_sem.at[2]),
         pltpu.make_async_copy(video_h, video, load_sem.at[3]),
@@ -120,11 +122,10 @@
             parts += [both[:, :chans], both[:, chans:]]
         return jnp.concatenate(parts, axis=0)
 
-    loads[0].wait()
-    loads[1].wait()
-    shard = [sw[tap] for tap in range(9)] + [tw[tap].astype(BF16) for tap in range(3)]
-    for pair in range(6):
-        wp[c, pair] = jnp.concatenate([shard[2 * pair], shard[2 * pair + 1]], axis=1)
+    for load in loads[:2]:
+        load.wait()
+    for pair in range(4):
+        wp[c, pair] = jnp.concatenate([sw[2 * pair], sw[2 * pair + 1]], axis=1)
     tm_waits(barrier, 2)
 
     def send(src, dst, ssem, rsem, device):
@@ -155,14 +156,19 @@
         return wp.at[owner, 4, :, pl.ds(head, 2 * chans - head)]
 
     at_y, at_core, at_x, at_z = (tm, ypart), (tm, core), (xpart, c), (zpart, c)
-    y_a = wsend(0, low_part(c, parity), at_y)
+    y_a = wsend(0, low_part(c, h), at_y)
     y_b = wsend(1, low_part(c, 2 + h), at_y)
     y_rest = wsend(2, rest_part(c), at_y)
+    for load in loads[2:4]:
+        load.wait()
+    first = tw[0].astype(BF16)
+    wp[c, 4] = jnp.concatenate([sw[8], first], axis=1)
+    wp[c, 5] = jnp.concatenate([tw[1].astype(BF16), tw[2].astype(BF16)], axis=1)
     y_head = wsend(3, head_part(c), at_y)
     own = wsend(8, wp.at[c, pl.ds(0, 5)], at_core)
     tm_signals(gate.at[0])
 
-    loads[2].wait()
+    loads[4].wait()
     own_cot = cot[...].astype(BF16)
     for q in range(2):
         cb[q * quarter : (q + 1) * quarter] = pack(own_cot[q * half : (q + 1) * half])
@@ -204,13 +210,39 @@
             for q in range(chunks):
                 far_copy(base, halo, q).wait_recv()
 
-    def far_done(base, halo):
+    def stash_copy(slot, own_ref, held, q):
+        part = pl.ds(q * chunk, chunk)
+        return pltpu.make_async_remote_copy(
+            src_ref=own_ref.at[part, :], dst_ref=held.at[part, :],
+            send_sem=halo_send.at[4 * chunks + slot], recv_sem=halo_recv.at[4 * chunks + slot],
+            device_id=(lax.rem(tm + n_tm + 4 * parity - 2, n_tm), c), device_id_type=MESH,
+        )
+
+    def forward_copy(base, held, halo, q):
+        part = pl.ds(q * chunk, chunk)
+        return pltpu.make_async_remote_copy(
+            src_ref=held.at[part, :], dst_ref=halo.at[1 - parity, part, :],
+            send_sem=halo_send.at[base + chunks + q], recv_sem=halo_recv.at[base + chunks + q],
+            device_id=at_x, device_id_type=MESH,
+        )
+
+    cot_stash = (0, cb, cstash), (1, cb, cstash)
+    hid_stash = (2, hpack, hstash), (3, hpack, hstash)
+
+    def stash_start(which, q):
+        @pl.when(gets_far)
+        def _():
+            stash_copy(*which, q).start()
+
+    def forward(base, which, halo, q):
         @pl.when(sends_far)
         def _():
-            for q in range(chunks):
-                far_copy(base, halo, q).wait_send()
-
-    cot_near = [near_send(0, cb, chalo, q) for q in range(2)]
+            stash_copy(*which, q).wait_recv()
+            forward_copy(base, which[2], halo, q).start()
+
+    cot_near = [near_send(0, cb, chalo, q) for q in range(chunks)]
+    for e in range(2):
+        stash_start(cot_stash[e], 2 + e)
 
     for edge, slot in ((0, 0), (n_tm - 1, 1)):
         @pl.when(tm == edge)
@@ -232,8 +264,8 @@
     for b in range(3):
         gpad[b, 0:width] = jnp.zeros((width, chans), BF16)
         gpad[b, width + rows :] = jnp.zeros((width, chans), BF16)
-    loads[3].wait()
-    loads[4].wait()
+    loads[5].wait()
+    loads[6].wait()
     frame = video[...]
     views = [shifted(frame, 1 - b).astype(BF16) for b in range(3)]
     for s in range(2):
@@ -247,14 +279,13 @@
         for e in taps:
             wg[2 * pair + e, band] = both[:, e * chans : (e + 1) * chans]
 
-    def unpack_spatial(owner):
-        for pair in range(4):
-            unpack_pair(owner, pair)
-        unpack_pair(owner, 4, (0,))
-
-    def conv_part(s, q):
+    def unpack_spatial(owner, first=0, count=5):
+        for pair in range(first, first + count):
+            unpack_pair(owner, pair, (0, 1) if pair < 4 else (0,))
+
+    def conv_part(s, q, taps=(0, 1, 2)):
         total = None
-        for a in range(3):
+        for a in taps:
             band = pl.ds(pl.multiple_of(s * side_chans, 16), side_chans)
             weights = jnp.concatenate([wg[3 * a + b, band] for b in range(3)], axis=0)
             term = nn_dot(
@@ -283,77 +314,54 @@
         spat[q * half : (q + 1) * half] = bias_ref[...].reshape(1, chans) + conv_part(yc, q)
 
     y_a.wait_recv()
-    x_a = wsend(6, low_part(ypart, parity), at_x)
-    r_a = wsend(10, low_part(ypart, parity), at_core)
-    cot_near += [near_send(0, cb, chalo, q) for q in range(2, chunks)]
-    cot_near[0].wait_recv()
-    far_start(0, chalo, 0)
+    z_a = wsend(6, low_part(ypart, h), at_z)
+    r_a = wsend(10, low_part(ypart, h), at_core)
     y_b.wait_recv()
     z_b = wsend(7, low_part(ypart, 2 + h), at_z)
     r_b = wsend(11, low_part(ypart, 2 + h), at_core)
-    cot_near[1].wait_recv()
-    far_start(0, chalo, 1)
     gate_step(0)
     y_rest.wait_recv()
     r_rest = wsend(12, rest_part(ypart), at_core)
-    y_tail = wsend(4, tail_part(c), at_y)
-    y_last = wsend(5, wp.at[c, 5], at_y)
-    own_last = wsend(9, wp.at[c, 5], at_core)
-    x_a.wait_recv()
-    r_x = wsend(14, low_part(ypart, 1 - parity), at_core)
+    z_a.wait_recv()
+    r_za = wsend(14, low_part(ypart, 1 - h), at_core)
     gate_step(1)
     y_head.wait_recv()
     r_head = wsend(13, head_part(ypart), at_core)
+    y_tail = wsend(4, tail_part(c), at_y)
+    y_last = wsend(5, wp.at[c, 5], at_y)
+    for q in range(2):
+        cot_near[q].wait_recv()
+        far_start(0, chalo, q)
     z_b.wait_recv()
-    r_z = wsend(15, low_part(ypart, 3 - h), at_core)
+    r_zb = wsend(15, low_part(ypart, 3 - h), at_core)
+    for e in range(2):
+        forward(0, cot_stash[e], chalo, 2 + e)
+    diagonal = flip(core, 2)
     unpack_spatial(ypart)
-    cot_near[2].wait_recv()
-    far_start(0, chalo, 2)
-    for copy in (r_a, r_b, r_rest, r_x, r_head, r_z):
+    for copy in (r_a, r_rest, r_za):
         copy.wait_recv()
-    unpack_spatial(flip(core, 2))
-
-    def stash_copy(q):
-        part = pl.ds(q * chunk, chunk)
-        return pltpu.make_async_remote_copy(
-            src_ref=hpack.at[part, :], dst_ref=stash.at[part, :],
-            send_sem=halo_send.at[4 * chunks + q], recv_sem=halo_recv.at[4 * chunks + q],
-            device_id=(lax.rem(tm + n_tm + 4 * parity - 2, n_tm), c), device_id_type=MESH,
-        )
-
-    def forward_copy(q):
-        part = pl.ds(q * chunk, chunk)
-        return pltpu.make_async_remote_copy(
-            src_ref=stash.at[part, :], dst_ref=hhalo.at[1 - parity, part, :],
-            send_sem=halo_send.at[3 * chunks + q], recv_sem=halo_recv.at[3 * chunks + q],
-            device_id=at_x, device_id_type=MESH,
-        )
-
-    def stash_hidden(q):
-        @pl.when(gets_far)
-        def _():
-            stash_copy(q).start()
-
-    def forward_hidden(q):
-        @pl.when(sends_far)
-        def _():
-            stash_copy(q).wait_recv()
-            forward_copy(q).start()
+    unpack_spatial(diagonal, 0, 2)
+    for q in range(2):
+        part = pl.ds(q * half, half)
+        spat[part] = spat[part] + conv_part(1 - yc, q, (0,))
+    for copy in (r_b, r_head, r_zb):
+        copy.wait_recv()
+    own_last = wsend(9, wp.at[c, 5], at_core)
+    unpack_spatial(diagonal, 2, 3)
 
     hid_near = []
     for q in range(2):
-        acc = spat[q * half : (q + 1) * half] + conv_part(1 - yc, q)
+        acc = spat[q * half : (q + 1) * half] + conv_part(1 - yc, q, (1, 2))
         hidden = (acc * jax.nn.sigmoid(acc)).astype(BF16)
         hb[q * half : (q + 1) * half] = hidden
         hpack[q * quarter : (q + 1) * quarter] = pack(hidden)
         hid_near += [near_send(2 * chunks, hpack, hhalo, 2 * q + e) for e in range(2)]
         if q == 1:
-            stash_hidden(2)
-            stash_hidden(3)
+            for e in range(2):
+                stash_start(hid_stash[e], 2 + e)
         spat[q * half : (q + 1) * half] = acc
-        if q == 0:
-            cot_near[3].wait_recv()
-            far_start(0, chalo, 3)
+    cot_near[2].wait_recv()
+    cot_near[3].wait_recv()
 
     early = (n_tm - n_early) * parity
     late = n_early * (1 - parity)
@@ -465,7 +473,6 @@
     core_e[1].wait_recv()
     y_e.wait_recv()
     scatter(early, n_early)
-    pass_hidden(1)
 
     def grad_conv(q):
         acc = cot[q * half : (q + 1) * half]
@@ -478,10 +485,11 @@
     core_l[1].wait_recv()
     y_l.wait_recv()
     scatter(late, n_late)
-    forward_hidden(2)
-    forward_hidden(3)
     grad_conv(0)
+    pass_hidden(1)
     grad_conv(1)
+    for e in range(2):
+        forward(2 * chunks, hid_stash[e], hhalo, 2 + e)
     out_v[...] = video[...] + nn_dot(hb[...], wg[10])
 
     @pl.when(owns)
@@ -518,19 +526,24 @@
 
     for copy in w_copies + cot_near + hid_near + core_e + core_l + [y_e, y_l]:
         copy.wait_send()
-    far_done(0, chalo)
 
     @pl.when(sends_far)
     def _():
         for q in range(2):
+            far_copy(0, chalo, q).wait_send()
+        for q in range(2, chunks):
+            forward_copy(0, cstash, chalo, q).wait_send()
+        for q in range(2):
             far_copy(2 * chunks, hhalo, q).wait_send()
         for q in range(2, chunks):
-            forward_copy(q).wait_send()
+            forward_copy(2 * chunks, hstash, hhalo, q).wait_send()
 
     @pl.when(gets_far)
     def _():
-        for q in range(2, chunks):
-            stash_copy(q).wait_send()
+        for e in range(2):
+            stash_copy(*cot_stash[e], 2 + e).wait_send()
+        for e in range(2):
+            stash_copy(*hid_stash[e], 2 + e).wait_send()
 
     for unit in range(n_tm):
         @pl.when(tm != first_owner + unit // share)
@@ -595,6 +608,7 @@
             vm((rows, n_tm * lanes - 2 * chans), BF16),
             vm((rows, chans), BF16),
             vm((rows // 2, 2 * chans), BF16),
+            vm((rows // 2, 2 * chans), BF16),
             vm((2, rows // 2, 2 * chans), BF16),
             vm((rows // 2, 2 * chans), BF16),
             vm((rows, chans), F32),
@@ -607,7 +621,7 @@
             vm((n_tm, depth, lanes), BF16),
             vm((n_tm, n_tm // 4, depth, lanes), BF16),
             vm((n_tm, depth, lanes), BF16),
-            dma((5,)),
+            dma((7,)),
             dma((18,)),
             dma((18,)),
             dma((20,)),

time: 38.2 us -> 37.1 us (0.971)
  Pallas kernels: 37.4 us -> 36.3 us
    pallas_call x1, Pallas kernels: 36 us -> 35 us  [fused(): pl.pallas_call(functools.partial(block_kernel, (n_tm, n_clip, height, wid...]
where the time goes in v3:
time: 37.1 us; the launch traced here: 37 us
  Pallas kernels  36.3 us (98%)
  between operations  0.64 us (2%)
    pallas_call x1, Pallas kernels, fused(): pl.pallas_call(functools.partial(block_kernel, (n_tm, n_clip, height, wid...  35 us
    pallas_call x1, Pallas kernels, fused(): pl.pallas_call(hand_over, out_shape=shapes, in_specs=[vm_spec] * 3, out_s...  1.36 us

profile of v3, /device:TPU:0, one launch (start us, length us, event | category | flops | bytes accessed | tf_op | source)
XLA Modules:
  0.0 37.0 jit_solution(9694497309960932115)
XLA Ops:
  0.6 35.0 %block.1 = (f32[512,320]{1,0:T(8,128)S(1)}, f32[512,320]{1,0:T(8,128)S(1)}, f32[3,80,320]{2,1,0:T(8,128)S(1)}) custom-call(f32[512,320]{1,0:T(8,128)} %bitcast.4, bf16[9,80,320]{2,1,0:T(8,128)(2,1)} %sw_h.1, f32[320]{0:T(512)} %bias_h.1, f32[3,80,320]{2,1,0:T(8,128)} %tw_h.1, f32[512,320]{1,0:T(8,128)} %bitcast.5), custom_call_target="tpu_custom_call" | custom-call | tf_op jit(solution)/shard_map/block/pallas_call | solution.py:587
  35.6 1.4 %hand_over.1 = (f32[512,320]{1,0:T(8,128)}, f32[512,320]{1,0:T(8,128)}, f32[3,80,320]{2,1,0:T(8,128)}) custom-call(f32[512,320]{1,0:T(8,128)S(1)} %get-tuple-element.9.refs_0_, f32[512,320]{1,0:T(8,128)S(1)} %get-tuple-element.10.refs_1_, f32[3,80,320]{2,1,0:T(8,128)S(1)} %get-tuple-element.11.refs_2_), custom_call_target="tpu_custom_call" | custom-call | tf_op jit(solution)/shard_map/hand_over/pallas_call | solution.py:645

commit v4 on v3

--- a/solution.py
+++ b/solution.py
@@ -102,8 +102,8 @@
 
     loads = [
         pltpu.make_async_copy(sw_h.at[pl.ds(0, 4)], sw.at[pl.ds(0, 4)], load_sem.at[0]),
-        pltpu.make_async_copy(sw_h.at[pl.ds(4, 4)], sw.at[pl.ds(4, 4)], load_sem.at[5]),
-        pltpu.make_async_copy(sw_h.at[pl.ds(8, 1)], sw.at[pl.ds(8, 1)], load_sem.at[6]),
+        pltpu.make_async_copy(sw_h.at[pl.ds(4, 4)], sw.at[pl.ds(4, 4)], load_sem.at[0]),
+        pltpu.make_async_copy(sw_h.at[pl.ds(8, 1)], sw.at[pl.ds(8, 1)], load_sem.at[5]),
         pltpu.make_async_copy(tw_h, tw, load_sem.at[1]),
         pltpu.make_async_copy(cot_h, cot, load_sem.at[2]),
         pltpu.make_async_copy(video_h, video, load_sem.at[3]),
@@ -122,8 +122,7 @@
             parts += [both[:, :chans], both[:, chans:]]
         return jnp.concatenate(parts, axis=0)
 
-    for load in loads[:2]:
-        load.wait()
+    pltpu.make_async_copy(sw_h.at[pl.ds(0, 8)], sw.at[pl.ds(0, 8)], load_sem.at[0]).wait()
     for pair in range(4):
         wp[c, pair] = jnp.concatenate([sw[2 * pair], sw[2 * pair + 1]], axis=1)
     tm_waits(barrier, 2)
@@ -136,12 +135,23 @@
         copy.start()
         return copy
 
-    w_copies = []
+    def settle(ref, ssem, rsem):
+        return pltpu.make_async_remote_copy(
+            src_ref=ref, dst_ref=ref, send_sem=ssem, recv_sem=rsem,
+            device_id=(tm, core), device_id_type=MESH,
+        )
+
+    def sent(ref, sem):
+        settle(ref, sem, sem).wait_send()
+
+    def received(ref, sem):
+        settle(ref, sem, sem).wait_recv()
+
+    def block_rows(count):
+        return chalo.at[0, pl.ds(0, count)]
 
     def wsend(slot, part, device):
-        copy = send(part, part, w_send.at[slot], w_recv.at[slot], device)
-        w_copies.append(copy)
-        return copy
+        return send(part, part, w_send.at[0], w_recv.at[slot], device)
 
     def low_part(owner, pair):
         return wp.at[owner, pair, pl.ds(0, low)]
@@ -173,21 +183,21 @@
     for q in range(2):
         cb[q * quarter : (q + 1) * quarter] = pack(own_cot[q * half : (q + 1) * half])
 
-    def near_send(base, own_ref, halo, q):
+    def near_send(which, own_ref, halo, q):
         part = pl.ds(q * chunk, chunk)
         return send(
             own_ref.at[part, :], halo.at[parity, part, :],
-            halo_send.at[base + q], halo_recv.at[base + q], (xpart, c),
-        )
-
-    def far_copy(base, halo, q):
+            halo_send.at[which], halo_recv.at[3 * which + min(q, 2)], (xpart, c),
+        )
+
+    def far_copy(which, halo, q):
         target = lax.rem(tm + n_tm + 2 - 4 * parity, n_tm)
         part = pl.ds(q * chunk, chunk)
         return pltpu.make_async_remote_copy(
             src_ref=halo.at[1 - parity, part, :],
             dst_ref=halo.at[parity, part, :],
-            send_sem=halo_send.at[base + chunks + q],
-            recv_sem=halo_recv.at[base + chunks + q],
+            send_sem=halo_send.at[2],
+            recv_sem=halo_recv.at[6 + which],
             device_id=(target, c),
             device_id_type=MESH,
         )
@@ -199,50 +209,41 @@
         jnp.logical_and(parity == 0, has_down), jnp.logical_and(parity == 1, has_up)
     )
 
-    def far_start(base, halo, q):
+    def far_start(which, halo, q):
         @pl.when(sends_far)
         def _():
-            far_copy(base, halo, q).start()
-
-    def far_recv(base, halo):
+            far_copy(which, halo, q).start()
+
+    def far_recv(which):
         @pl.when(gets_far)
         def _():
-            for q in range(chunks):
-                far_copy(base, halo, q).wait_recv()
-
-    def stash_copy(slot, own_ref, held, q):
-        part = pl.ds(q * chunk, chunk)
-        return pltpu.make_async_remote_copy(
-            src_ref=own_ref.at[part, :], dst_ref=held.at[part, :],
-            send_sem=halo_send.at[4 * chunks + slot], recv_sem=halo_recv.at[4 * chunks + slot],
-            device_id=(lax.rem(tm + n_tm + 4 * parity - 2, n_tm), c), device_id_type=MESH,
-        )
-
-    def forward_copy(base, held, halo, q):
-        part = pl.ds(q * chunk, chunk)
-        return pltpu.make_async_remote_copy(
-            src_ref=held.at[part, :], dst_ref=halo.at[1 - parity, part, :],
-            send_sem=halo_send.at[base + chunks + q], recv_sem=halo_recv.at[base + chunks + q],
-            device_id=at_x, device_id_type=MESH,
-        )
-
-    cot_stash = (0, cb, cstash), (1, cb, cstash)
-    hid_stash = (2, hpack, hstash), (3, hpack, hstash)
-
-    def stash_start(which, q):
+            received(block_rows(half), halo_recv.at[6 + which])
+
+    def stash_start(which, own_ref, held):
         @pl.when(gets_far)
         def _():
-            stash_copy(*which, q).start()
-
-    def forward(base, which, halo, q):
+            for q in range(2, chunks):
+                part = pl.ds(q * chunk, chunk)
+                pltpu.make_async_remote_copy(
+                    src_ref=own_ref.at[part, :], dst_ref=held.at[part, :],
+                    send_sem=halo_send.at[3], recv_sem=halo_recv.at[8 + which],
+                    device_id=(lax.rem(tm + n_tm + 4 * parity - 2, n_tm), c), device_id_type=MESH,
+                ).start()
+
+    def forward(which, held, halo):
         @pl.when(sends_far)
         def _():
-            stash_copy(*which, q).wait_recv()
-            forward_copy(base, which[2], halo, q).start()
+            received(block_rows(2 * chunk), halo_recv.at[8 + which])
+            for q in range(2, chunks):
+                part = pl.ds(q * chunk, chunk)
+                pltpu.make_async_remote_copy(
+                    src_ref=held.at[part, :], dst_ref=halo.at[1 - parity, part, :],
+                    send_sem=halo_send.at[2], recv_sem=halo_recv.at[6 + which],
+                    device_id=at_x, device_id_type=MESH,
+                ).start()
 
     cot_near = [near_send(0, cb, chalo, q) for q in range(chunks)]
-    for e in range(2):
-        stash_start(cot_stash[e], 2 + e)
+    stash_start(0, cb, cstash)
 
     for edge, slot in ((0, 0), (n_tm - 1, 1)):
         @pl.when(tm == edge)
@@ -315,38 +316,36 @@
 
     y_a.wait_recv()
     z_a = wsend(6, low_part(ypart, h), at_z)
-    r_a = wsend(10, low_part(ypart, h), at_core)
+    wsend(9, low_part(ypart, h), at_core)
     y_b.wait_recv()
     z_b = wsend(7, low_part(ypart, 2 + h), at_z)
-    r_b = wsend(11, low_part(ypart, 2 + h), at_core)
+    wsend(10, low_part(ypart, 2 + h), at_core)
     gate_step(0)
     y_rest.wait_recv()
-    r_rest = wsend(12, rest_part(ypart), at_core)
+    wsend(9, rest_part(ypart), at_core)
     z_a.wait_recv()
-    r_za = wsend(14, low_part(ypart, 1 - h), at_core)
+    wsend(9, low_part(ypart, 1 - h), at_core)
     gate_step(1)
     y_head.wait_recv()
-    r_head = wsend(13, head_part(ypart), at_core)
+    wsend(10, head_part(ypart), at_core)
     y_tail = wsend(4, tail_part(c), at_y)
     y_last = wsend(5, wp.at[c, 5], at_y)
     for q in range(2):
         cot_near[q].wait_recv()
         far_start(0, chalo, q)
     z_b.wait_recv()
-    r_zb = wsend(15, low_part(ypart, 3 - h), at_core)
-    for e in range(2):
-        forward(0, cot_stash[e], chalo, 2 + e)
+    wsend(10, low_part(ypart, 3 - h), at_core)
+    forward(0, cstash, chalo)
     diagonal = flip(core, 2)
     unpack_spatial(ypart)
-    for copy in (r_a, r_rest, r_za):
-        copy.wait_recv()
+    received(block_rows(4 * depth - 2 * low), w_recv.at[9])
     unpack_spatial(diagonal, 0, 2)
     for q in range(2):
         part = pl.ds(q * half, half)
         spat[part] = spat[part] + conv_part(1 - yc, q, (0,))
-    for copy in (r_b, r_head, r_zb):
-        copy.wait_recv()
-    own_last = wsend(9, wp.at[c, 5], at_core)
+    head_rows = depth * head // (2 * chans)
+    received(block_rows(2 * low + head_rows), w_recv.at[10])
+    wsend(11, wp.at[c, 5], at_core)
     unpack_spatial(diagonal, 2, 3)
 
     hid_near = []
@@ -355,13 +354,11 @@
         hidden = (acc * jax.nn.sigmoid(acc)).astype(BF16)
         hb[q * half : (q + 1) * half] = hidden
         hpack[q * quarter : (q + 1) * quarter] = pack(hidden)
-        hid_near += [near_send(2 * chunks, hpack, hhalo, 2 * q + e) for e in range(2)]
+        hid_near += [near_send(1, hpack, hhalo, 2 * q + e) for e in range(2)]
         if q == 1:
-            for e in range(2):
-                stash_start(hid_stash[e], 2 + e)
+            stash_start(1, hpack, hstash)
         spat[q * half : (q + 1) * half] = acc
-    cot_near[2].wait_recv()
-    cot_near[3].wait_recv()
+    received(block_rows(2 * chunk), halo_recv.at[2])
 
     early = (n_tm - n_early) * parity
     late = n_early * (1 - parity)
@@ -377,14 +374,14 @@
         part = pl.ds(first, count)
         return send(
             gtl.at[1 - mine, side, part], rx.at[side, part],
-            g_send.at[slot], g_recv.at[slot], at_core,
+            g_send.at[0], g_recv.at[slot], at_core,
         )
 
     def y_send(slot, first, count):
         for i in range(count):
             ysend[first + i] = (gtl[mine, 1 - yc, first + i] + rx[1 - yc, first + i]).astype(BF16)
         part = pl.ds(first, count)
-        return send(ysend.at[part], ry.at[part], g_send.at[slot], g_recv.at[slot], at_y)
+        return send(ysend.at[part], ry.at[part], g_send.at[1], g_recv.at[slot], at_y)
 
     share = n_tm // 4
     first_owner = n_tm // 2 - 2
@@ -394,22 +391,15 @@
         place_in = lax.rem(unit, share)
         return pltpu.make_async_remote_copy(
             src_ref=pb.at[unit], dst_ref=rs.at[tm, place_in],
-            send_sem=a_send.at[unit], recv_sem=a_recv.at[tm * share + place_in],
+            send_sem=a_send.at[0], recv_sem=a_recv.at[0],
             device_id=(first_owner + unit // share, c), device_id_type=MESH,
-        )
-
-    def arrival(sender, place_in):
-        return pltpu.make_async_remote_copy(
-            src_ref=pb.at[place_in], dst_ref=rs.at[sender, place_in], send_sem=a_send.at[place_in],
-            recv_sem=a_recv.at[sender * share + place_in],
-            device_id=(sender, c), device_id_type=MESH,
         )
 
     def gather_copy(owner, to):
         part = ag.at[pl.ds(owner * share, share)]
         return pltpu.make_async_remote_copy(
             src_ref=part, dst_ref=part,
-            send_sem=a_send.at[n_tm + to], recv_sem=a_recv.at[n_tm * share + owner],
+            send_sem=a_send.at[1], recv_sem=a_recv.at[1],
             device_id=(to, c), device_id_type=MESH,
         )
 
@@ -426,7 +416,7 @@
 
     def pass_hidden(q):
         hid_near[q].wait_recv()
-        far_start(2 * chunks, hhalo, q)
+        far_start(1, hhalo, q)
 
     @pl.when(parity == 0)
     def _():
@@ -441,21 +431,20 @@
     core_e[0].wait_recv()
     y_e = y_send(4, early, n_early)
 
-    far_recv(0, chalo)
+    far_recv(0)
     cotl[:, 0:chans] = unpack(chalo, parity)
     place(outer_dot(hb[...], cotl[...]), late, n_late)
     core_l = [core_send(2 + e, side, late, n_late) for e, side in enumerate((1 - yc, yc))]
 
     y_tail.wait_recv()
-    r_tail = wsend(16, tail_part(ypart), at_core)
+    wsend(11, tail_part(ypart), at_core)
     y_last.wait_recv()
-    r_last = wsend(17, wp.at[ypart, 5], at_core)
+    wsend(11, wp.at[ypart, 5], at_core)
     pass_hidden(0)
     core_l[0].wait_recv()
     y_l = y_send(5, late, n_late)
 
-    for copy in (own_last, r_tail, r_last):
-        copy.wait_recv()
+    received(block_rows(3 * depth - head_rows), w_recv.at[11])
     for owner in range(n_clip):
         unpack_pair(owner, 4, (1,))
         unpack_pair(owner, 5)
@@ -488,19 +477,14 @@
     grad_conv(0)
     pass_hidden(1)
     grad_conv(1)
-    for e in range(2):
-        forward(2 * chunks, hid_stash[e], hhalo, 2 + e)
+    forward(1, hstash, hhalo)
     out_v[...] = video[...] + nn_dot(hb[...], wg[10])
 
     @pl.when(owns)
     def _():
         mine_at = tm - first_owner
         rs[tm] = jnp.zeros(rs.shape[1:], BF16)
-        for sender in range(n_tm):
-            @pl.when(tm != sender)
-            def _():
-                for e in range(share):
-                    arrival(sender, e).wait_recv()
+        received(rs.at[pl.ds(0, n_tm - 1)], a_recv.at[0])
         for e in range(share):
             total = psum[mine_at * share + e]
             for sender in range(n_tm):
@@ -511,51 +495,44 @@
             def _():
                 gather_copy(mine_at, to).start()
 
-    far_recv(2 * chunks, hhalo)
-    hid_near[2].wait_recv()
-    hid_near[3].wait_recv()
+    far_recv(1)
+    received(block_rows(2 * chunk), halo_recv.at[5])
     out_v[...] = out_v[...] + nn_dot(unpack(hhalo, 0), wg[9]) + nn_dot(unpack(hhalo, 1), wg[11])
 
-    for owner in range(4):
-        @pl.when(tm != first_owner + owner)
-        def _():
-            gather_copy(owner, tm).wait_recv()
+    @pl.when(owns)
+    def _():
+        received(ag.at[pl.ds(0, 3 * share)], a_recv.at[1])
+
+    @pl.when(jnp.logical_not(owns))
+    def _():
+        received(ag, a_recv.at[1])
+
     whole = jnp.concatenate([ag[to] for to in range(n_tm)], axis=1).astype(F32) * scale
     for k in range(3):
         gt_v[k] = whole[:, k * chans : (k + 1) * chans]
 
-    for copy in w_copies + cot_near + hid_near + core_e + core_l + [y_e, y_l]:
-        copy.wait_send()
+    sent(wp.at[pl.ds(0, 3)], w_send.at[0])
+    sent(block_rows(half), halo_send.at[0])
+    sent(block_rows(half), halo_send.at[1])
+    sent(gtl.at[0], g_send.at[0])
+    sent(ysend, g_send.at[1])
 
     @pl.when(sends_far)
     def _():
-        for q in range(2):
-            far_copy(0, chalo, q).wait_send()
-        for q in range(2, chunks):
-            forward_copy(0, cstash, chalo, q).wait_send()
-        for q in range(2):
-            far_copy(2 * chunks, hhalo, q).wait_send()
-        for q in range(2, chunks):
-            forward_copy(2 * chunks, hstash, hhalo, q).wait_send()
+        sent(chalo, halo_send.at[2])
 
     @pl.when(gets_far)
     def _():
-        for e in range(2):
-            stash_copy(*cot_stash[e], 2 + e).wait_send()
-        for e in range(2):
-            stash_copy(*hid_stash[e], 2 + e).wait_send()
-
-    for unit in range(n_tm):
-        @pl.when(tm != first_owner + unit // share)
-        def _():
-            scatter_copy(unit).wait_send()
+        sent(block_rows(half), halo_send.at[3])
 
     @pl.when(owns)
     def _():
-        for to in range(n_tm):
-            @pl.when(tm != to)
-            def _():
-                gather_copy(tm - first_owner, to).wait_send()
+        sent(pb.at[pl.ds(0, n_tm - share)], a_send.at[0])
+        sent(rs.at[pl.ds(0, n_tm - 1)], a_send.at[1])
+
+    @pl.when(jnp.logical_not(owns))
+    def _():
+        sent(pb, a_send.at[0])
 
 
 def hand_over(*refs):
@@ -563,11 +540,7 @@
     ins, outs, sem = refs[:n], refs[n : 2 * n], refs[2 * n]
     writes = []
     for e in range(n):
-        extent = ins[e].shape[0]
-        count = 4 if extent % 64 == 0 else 1
-        for q in range(count):
-            part = pl.ds(q * (extent // count), extent // count)
-            writes.append(pltpu.make_async_copy(ins[e].at[part], outs[e].at[part], sem.at[4 * e + q]))
+        writes.append(pltpu.make_async_copy(ins[e], outs[e], sem.at[e]))
     for write in writes:
         write.start()
     for write in writes:
@@ -621,15 +594,15 @@
             vm((n_tm, depth, lanes), BF16),
             vm((n_tm, n_tm // 4, depth, lanes), BF16),
             vm((n_tm, depth, lanes), BF16),
-            dma((7,)),
-            dma((18,)),
-            dma((18,)),
-            dma((20,)),
-            dma((20,)),
             dma((6,)),
+            dma((1,)),
+            dma((12,)),
+            dma((4,)),
+            dma((10,)),
+            dma((2,)),
             dma((6,)),
-            dma((2 * n_tm,)),
-            dma((n_tm * (n_tm // 4) + 4,)),
+            dma((2,)),
+            dma((2,)),
             pltpu.SemaphoreType.REGULAR((n_tm // 2 - 1,)),
         ],
         compiler_params=pltpu.CompilerParams(
@@ -647,7 +620,7 @@
         out_shape=shapes,
         in_specs=[vm_spec] * 3,
         out_specs=(any_spec,) * 3,
-        scratch_shapes=[dma((12,))],
+        scratch_shapes=[dma((3,))],
         compiler_params=pltpu.CompilerParams(vmem_limit_bytes=2**20),
         name="hand_over",
     )(*results)
@@ -726,8 +699,9 @@
         one_frame = video.shape[0] == 1 and video.shape[1] == 1
         depth, chans = spatial_w.shape[1:]
         lanes = -(-3 * chans // (128 * n_tm)) * 128
+        whole_rows = depth * (-(-chans // 128) * 128) % (2 * chans) == 0
         fits = depth % 16 == 0 and depth > 16 * TAIL and 2 * chans % lanes == 0
-        if one_frame and fits and n_clip == 4 and n_tm % 4 == 0 and n_tm * lanes <= 4 * chans:
+        if one_frame and fits and n_clip == 4 and n_tm % 4 == 0 and n_tm * lanes <= 4 * chans and whole_rows:
             return fused(n_tm, n_clip, *args)
         return native(*args)
 

time: 37.1 us -> 36.2 us (0.976)
  Pallas kernels: 36.3 us -> 35.4 us
    pallas_call x1, Pallas kernels: 35 us -> 34.1 us  [fused(): pl.pallas_call(functools.partial(block_kernel, (n_tm, n_clip, height, wid...]
where the time goes in v4:
time: 36.2 us; the launch traced here: 36.1 us
  Pallas kernels  35.4 us (98%)
  between operations  0.64 us (2%)
    pallas_call x1, Pallas kernels, fused(): pl.pallas_call(functools.partial(block_kernel, (n_tm, n_clip, height, wid...  34.1 us
    pallas_call x1, Pallas kernels, fused(): pl.pallas_call(hand_over, out_shape=shapes, in_specs=[vm_spec] * 3, out_s...  1.28 us

profile of v4, /device:TPU:0, one launch (start us, length us, event | category | flops | bytes accessed | tf_op | source)
XLA Modules:
  0.0 36.1 jit_solution(860332530723607319)
XLA Ops:
  0.6 34.1 %block.1 = (f32[512,320]{1,0:T(8,128)S(1)}, f32[512,320]{1,0:T(8,128)S(1)}, f32[3,80,320]{2,1,0:T(8,128)S(1)}) custom-call(f32[512,320]{1,0:T(8,128)} %bitcast.4, bf16[9,80,320]{2,1,0:T(8,128)(2,1)} %sw_h.1, f32[320]{0:T(512)} %bias_h.1, f32[3,80,320]{2,1,0:T(8,128)} %tw_h.1, f32[512,320]{1,0:T(8,128)} %bitcast.5), custom_call_target="tpu_custom_call" | custom-call | tf_op jit(solution)/shard_map/block/pallas_call | solution.py:560
  34.8 1.3 %hand_over.1 = (f32[512,320]{1,0:T(8,128)}, f32[512,320]{1,0:T(8,128)}, f32[3,80,320]{2,1,0:T(8,128)}) custom-call(f32[512,320]{1,0:T(8,128)S(1)} %get-tuple-element.9.refs_0_, f32[512,320]{1,0:T(8,128)S(1)} %get-tuple-element.10.refs_1_, f32[3,80,320]{2,1,0:T(8,128)S(1)} %get-tuple-element.11.refs_2_), custom_call_target="tpu_custom_call" | custom-call | tf_op jit(solution)/shard_map/hand_over/pallas_call | solution.py:618

commit v5 on v4

--- a/solution.py
+++ b/solution.py
@@ -323,6 +323,7 @@
     gate_step(0)
     y_rest.wait_recv()
     wsend(9, rest_part(ypart), at_core)
+    forward(0, cstash, chalo)
     z_a.wait_recv()
     wsend(9, low_part(ypart, 1 - h), at_core)
     gate_step(1)
@@ -335,7 +336,6 @@
         far_start(0, chalo, q)
     z_b.wait_recv()
     wsend(10, low_part(ypart, 3 - h), at_core)
-    forward(0, cstash, chalo)
     diagonal = flip(core, 2)
     unpack_spatial(ypart)
     received(block_rows(4 * depth - 2 * low), w_recv.at[9])
@@ -440,9 +440,9 @@
     wsend(11, tail_part(ypart), at_core)
     y_last.wait_recv()
     wsend(11, wp.at[ypart, 5], at_core)
-    pass_hidden(0)
     core_l[0].wait_recv()
     y_l = y_send(5, late, n_late)
+    pass_hidden(0)
 
     received(block_rows(3 * depth - head_rows), w_recv.at[11])
     for owner in range(n_clip):
@@ -495,9 +495,10 @@
             def _():
                 gather_copy(mine_at, to).start()
 
+    received(block_rows(2 * chunk), halo_recv.at[5])
+    out_v[...] = out_v[...] + nn_dot(unpack(hhalo, 1 - parity), wg[11 - 2 * parity])
     far_recv(1)
-    received(block_rows(2 * chunk), halo_recv.at[5])
-    out_v[...] = out_v[...] + nn_dot(unpack(hhalo, 0), wg[9]) + nn_dot(unpack(hhalo, 1), wg[11])
+    out_v[...] = out_v[...] + nn_dot(unpack(hhalo, parity), wg[9 + 2 * parity])
 
     @pl.when(owns)
     def _():

time: 36.2 us -> 35.9 us (level)
  no operation moved by 1% of the time
where the time goes in v5:
time: 35.9 us; the launch traced here: 35.8 us
  Pallas kernels  35.1 us (98%)
  between operations  0.64 us (2%)
    pallas_call x1, Pallas kernels, fused(): pl.pallas_call(functools.partial(block_kernel, (n_tm, n_clip, height, wid...  33.8 us
    pallas_call x1, Pallas kernels, fused(): pl.pallas_call(hand_over, out_shape=shapes, in_specs=[vm_spec] * 3, out_s...  1.28 us

profile of v5, /device:TPU:0, one launch (start us, length us, event | category | flops | bytes accessed | tf_op | source)
XLA Modules:
  0.0 35.8 jit_solution(2856605784571837496)
XLA Ops:
  0.6 33.8 %block.1 = (f32[512,320]{1,0:T(8,128)S(1)}, f32[512,320]{1,0:T(8,128)S(1)}, f32[3,80,320]{2,1,0:T(8,128)S(1)}) custom-call(f32[512,320]{1,0:T(8,128)} %bitcast.4, bf16[9,80,320]{2,1,0:T(8,128)(2,1)} %sw_h.1, f32[320]{0:T(512)} %bias_h.1, f32[3,80,320]{2,1,0:T(8,128)} %tw_h.1, f32[512,320]{1,0:T(8,128)} %bitcast.5), custom_call_target="tpu_custom_call" | custom-call | tf_op jit(solution)/shard_map/block/pallas_call | solution.py:561
  34.5 1.3 %hand_over.1 = (f32[512,320]{1,0:T(8,128)}, f32[512,320]{1,0:T(8,128)}, f32[3,80,320]{2,1,0:T(8,128)}) custom-call(f32[512,320]{1,0:T(8,128)S(1)} %get-tuple-element.9.refs_0_, f32[512,320]{1,0:T(8,128)S(1)} %get-tuple-element.10.refs_1_, f32[3,80,320]{2,1,0:T(8,128)S(1)} %get-tuple-element.11.refs_2_), custom_call_target="tpu_custom_call" | custom-call | tf_op jit(solution)/shard_map/hand_over/pallas_call | solution.py:619

commit v6 on v5

--- a/solution.py
+++ b/solution.py
@@ -327,30 +327,47 @@
     z_a.wait_recv()
     wsend(9, low_part(ypart, 1 - h), at_core)
     gate_step(1)
-    y_head.wait_recv()
-    wsend(10, head_part(ypart), at_core)
-    y_tail = wsend(4, tail_part(c), at_y)
-    y_last = wsend(5, wp.at[c, 5], at_y)
+    diagonal = flip(core, 2)
+    head_rows = depth * head // (2 * chans)
+
+    def later(slot, part):
+        return pltpu.make_async_remote_copy(
+            src_ref=part, dst_ref=part, send_sem=w_send.at[0], recv_sem=w_recv.at[slot],
+            device_id=at_y, device_id_type=MESH,
+        )
+
+    y_tail, y_last = later(4, tail_part(c)), later(5, wp.at[c, 5])
+
+    def pass_head(which):
+        @pl.when(mine == which)
+        def _():
+            y_head.wait_recv()
+            wsend(12, head_part(ypart), at_core)
+            y_tail.start()
+            y_last.start()
+
+    pass_head(1)
+    z_b.wait_recv()
+    wsend(10, low_part(ypart, 3 - h), at_core)
     for q in range(2):
         cot_near[q].wait_recv()
         far_start(0, chalo, q)
-    z_b.wait_recv()
-    wsend(10, low_part(ypart, 3 - h), at_core)
-    diagonal = flip(core, 2)
-    unpack_spatial(ypart)
+    unpack_spatial(ypart, 0, 4)
     received(block_rows(4 * depth - 2 * low), w_recv.at[9])
-    unpack_spatial(diagonal, 0, 2)
+    received(block_rows(2 * low), w_recv.at[10])
+    unpack_spatial(diagonal, 0, 4)
+    pass_head(0)
     for q in range(2):
         part = pl.ds(q * half, half)
-        spat[part] = spat[part] + conv_part(1 - yc, q, (0,))
-    head_rows = depth * head // (2 * chans)
-    received(block_rows(2 * low + head_rows), w_recv.at[10])
+        spat[part] = spat[part] + conv_part(1 - yc, q, (0, 1))
     wsend(11, wp.at[c, 5], at_core)
-    unpack_spatial(diagonal, 2, 3)
+    unpack_spatial(ypart, 4, 1)
+    received(block_rows(head_rows), w_recv.at[12])
+    unpack_spatial(diagonal, 4, 1)
 
     hid_near = []
     for q in range(2):
-        acc = spat[q * half : (q + 1) * half] + conv_part(1 - yc, q, (1, 2))
+        acc = spat[q * half : (q + 1) * half] + conv_part(1 - yc, q, (2,))
         hidden = (acc * jax.nn.sigmoid(acc)).astype(BF16)
         hb[q * half : (q + 1) * half] = hidden
         hpack[q * quarter : (q + 1) * quarter] = pack(hidden)
@@ -597,7 +614,7 @@
             vm((n_tm, depth, lanes), BF16),
             dma((6,)),
             dma((1,)),
-            dma((12,)),
+            dma((13,)),
             dma((4,)),
             dma((10,)),
             dma((2,)),

time: 35.9 us -> 35.7 us (level)
  no operation moved by 1% of the time
where the time goes in v6:
time: 35.7 us; the launch traced here: 35.5 us
  Pallas kernels  34.9 us (98%)
  between operations  0.64 us (2%)
    pallas_call x1, Pallas kernels, fused(): pl.pallas_call(functools.partial(block_kernel, (n_tm, n_clip, height, wid...  33.6 us
    pallas_call x1, Pallas kernels, fused(): pl.pallas_call(hand_over, out_shape=shapes, in_specs=[vm_spec] * 3, out_s...  1.28 us

profile of v6, /device:TPU:0, one launch (start us, length us, event | category | flops | bytes accessed | tf_op | source)
XLA Modules:
  0.0 35.5 jit_solution(11353474784771952434)
XLA Ops:
  0.6 33.6 %block.1 = (f32[512,320]{1,0:T(8,128)S(1)}, f32[512,320]{1,0:T(8,128)S(1)}, f32[3,80,320]{2,1,0:T(8,128)S(1)}) custom-call(f32[512,320]{1,0:T(8,128)} %bitcast.4, bf16[9,80,320]{2,1,0:T(8,128)(2,1)} %sw_h.1, f32[320]{0:T(512)} %bias_h.1, f32[3,80,320]{2,1,0:T(8,128)} %tw_h.1, f32[512,320]{1,0:T(8,128)} %bitcast.5), custom_call_target="tpu_custom_call" | custom-call | tf_op jit(solution)/shard_map/block/pallas_call | solution.py:578
  34.2 1.3 %hand_over.1 = (f32[512,320]{1,0:T(8,128)}, f32[512,320]{1,0:T(8,128)}, f32[3,80,320]{2,1,0:T(8,128)}) custom-call(f32[512,320]{1,0:T(8,128)S(1)} %get-tuple-element.9.refs_0_, f32[512,320]{1,0:T(8,128)S(1)} %get-tuple-element.10.refs_1_, f32[3,80,320]{2,1,0:T(8,128)S(1)} %get-tuple-element.11.refs_2_), custom_call_target="tpu_custom_call" | custom-call | tf_op jit(solution)/shard_map/hand_over/pallas_call | solution.py:636

commit v7 on v6

--- a/solution.py
+++ b/solution.py
@@ -362,6 +362,16 @@
         spat[part] = spat[part] + conv_part(1 - yc, q, (0, 1))
     wsend(11, wp.at[c, 5], at_core)
     unpack_spatial(ypart, 4, 1)
+    received(block_rows(2 * chunk), halo_recv.at[2])
+
+    @pl.when(parity == 0)
+    def _():
+        cote[:, 0:chans] = unpack(chalo, 1)
+
+    @pl.when(parity == 1)
+    def _():
+        cote[:, chans - skip : 2 * chans - skip] = unpack(chalo, 0)
+
     received(block_rows(head_rows), w_recv.at[12])
     unpack_spatial(diagonal, 4, 1)
 
@@ -375,7 +385,6 @@
         if q == 1:
             stash_start(1, hpack, hstash)
         spat[q * half : (q + 1) * half] = acc
-    received(block_rows(2 * chunk), halo_recv.at[2])
 
     early = (n_tm - n_early) * parity
     late = n_early * (1 - parity)
@@ -434,14 +443,6 @@
     def pass_hidden(q):
         hid_near[q].wait_recv()
         far_start(1, hhalo, q)
-
-    @pl.when(parity == 0)
-    def _():
-        cote[:, 0:chans] = unpack(chalo, 1)
-
-    @pl.when(parity == 1)
-    def _():
-        cote[:, chans - skip : 2 * chans - skip] = unpack(chalo, 0)
 
     place(outer_dot(hb[...], cote[...]), early, n_early)
     core_e = [core_send(e, side, early, n_early) for e, side in enumerate((1 - yc, yc))]

time: 35.7 us -> 35.8 us (level)
  no operation moved by 1% of the time
where the time goes in v7:
time: 35.8 us; the launch traced here: 35.7 us
  Pallas kernels  35 us (98%)
  between operations  0.64 us (2%)
    pallas_call x1, Pallas kernels, fused(): pl.pallas_call(functools.partial(block_kernel, (n_tm, n_clip, height, wid...  33.7 us
    pallas_call x1, Pallas kernels, fused(): pl.pallas_call(hand_over, out_shape=shapes, in_specs=[vm_spec] * 3, out_s...  1.28 us

profile of v7, /device:TPU:0, one launch (start us, length us, event | category | flops | bytes accessed | tf_op | source)
XLA Modules:
  0.0 35.7 jit_solution(5794298369634291204)
XLA Ops:
  0.6 33.7 %block.1 = (f32[512,320]{1,0:T(8,128)S(1)}, f32[512,320]{1,0:T(8,128)S(1)}, f32[3,80,320]{2,1,0:T(8,128)S(1)}) custom-call(f32[512,320]{1,0:T(8,128)} %bitcast.4, bf16[9,80,320]{2,1,0:T(8,128)(2,1)} %sw_h.1, f32[320]{0:T(512)} %bias_h.1, f32[3,80,320]{2,1,0:T(8,128)} %tw_h.1, f32[512,320]{1,0:T(8,128)} %bitcast.5), custom_call_target="tpu_custom_call" | custom-call | tf_op jit(solution)/shard_map/block/pallas_call | solution.py:579
  34.4 1.3 %hand_over.1 = (f32[512,320]{1,0:T(8,128)}, f32[512,320]{1,0:T(8,128)}, f32[3,80,320]{2,1,0:T(8,128)}) custom-call(f32[512,320]{1,0:T(8,128)S(1)} %get-tuple-element.9.refs_0_, f32[512,320]{1,0:T(8,128)S(1)} %get-tuple-element.10.refs_1_, f32[3,80,320]{2,1,0:T(8,128)S(1)} %get-tuple-element.11.refs_2_), custom_call_target="tpu_custom_call" | custom-call | tf_op jit(solution)/shard_map/hand_over/pallas_call | solution.py:637

commit v8 on v6

--- a/solution.py
+++ b/solution.py
@@ -95,11 +95,6 @@
         if r + 1 < rounds:
             tm_signals(gate.at[r + 1])
 
-    barrier = pltpu.get_barrier_semaphore()
-    signal(barrier, (tm, ypart))
-    signal(barrier, (tm, core))
-    tm_signals(barrier)
-
     loads = [
         pltpu.make_async_copy(sw_h.at[pl.ds(0, 4)], sw.at[pl.ds(0, 4)], load_sem.at[0]),
         pltpu.make_async_copy(sw_h.at[pl.ds(4, 4)], sw.at[pl.ds(4, 4)], load_sem.at[0]),
@@ -111,6 +106,11 @@
     ]
     for load in loads:
         load.start()
+
+    barrier = pltpu.get_barrier_semaphore()
+    signal(barrier, (tm, ypart))
+    signal(barrier, (tm, core))
+    tm_signals(barrier)
 
     def pack(value):
         return jnp.concatenate([value[:quarter], value[quarter:]], axis=1)

time: 35.7 us -> 35.6 us (level)
  no operation moved by 1% of the time
where the time goes in v8:
time: 35.6 us; the launch traced here: 35.5 us
  Pallas kernels  34.8 us (98%)
  between operations  0.64 us (2%)
    pallas_call x1, Pallas kernels, fused(): pl.pallas_call(functools.partial(block_kernel, (n_tm, n_clip, height, wid...  33.6 us
    pallas_call x1, Pallas kernels, fused(): pl.pallas_call(hand_over, out_shape=shapes, in_specs=[vm_spec] * 3, out_s...  1.28 us

profile of v8, /device:TPU:0, one launch (start us, length us, event | category | flops | bytes accessed | tf_op | source)
XLA Modules:
  0.0 35.5 jit_solution(9245762415383746912)
XLA Ops:
  0.6 33.6 %block.1 = (f32[512,320]{1,0:T(8,128)S(1)}, f32[512,320]{1,0:T(8,128)S(1)}, f32[3,80,320]{2,1,0:T(8,128)S(1)}) custom-call(f32[512,320]{1,0:T(8,128)} %bitcast.4, bf16[9,80,320]{2,1,0:T(8,128)(2,1)} %sw_h.1, f32[320]{0:T(512)} %bias_h.1, f32[3,80,320]{2,1,0:T(8,128)} %tw_h.1, f32[512,320]{1,0:T(8,128)} %bitcast.5), custom_call_target="tpu_custom_call" | custom-call | tf_op jit(solution)/shard_map/block/pallas_call | solution.py:578
  34.2 1.3 %hand_over.1 = (f32[512,320]{1,0:T(8,128)}, f32[512,320]{1,0:T(8,128)}, f32[3,80,320]{2,1,0:T(8,128)}) custom-call(f32[512,320]{1,0:T(8,128)S(1)} %get-tuple-element.9.refs_0_, f32[512,320]{1,0:T(8,128)S(1)} %get-tuple-element.10.refs_1_, f32[3,80,320]{2,1,0:T(8,128)S(1)} %get-tuple-element.11.refs_2_), custom_call_target="tpu_custom_call" | custom-call | tf_op jit(solution)/shard_map/hand_over/pallas_call | solution.py:636
